TPU v7x, 32 devices: a whole 2x2x4 slice. The times are simulated.
32 devices in a mesh: dp: 4 (over z), expert: 8 (over y, x, core).
Axes of the slice: x: 2, y: 2, z: 4, core: 2. Of those that a mesh axis runs over, the one named last changes fastest.
Arguments:
- grad_parts: bfloat16 [4, 32, 128, 2048], P('dp', 'expert'), may hold values from -6 to 6
- first_moment: float32 [32, 128, 2048], P('expert', None, 'dp'), may hold values from -4 to 4
- second_moment: float32 [32, 128, 2048], P('expert', None, 'dp'), may hold values from 0.05 to 2
- master_weight: float32 [32, 128, 2048], P('expert', None, 'dp'), may hold values from -6 to 6
- old_owner: int32 [28], replicated, may hold values from 0 to 6, as said below
- new_owner: int32 [28], replicated, may hold values from 0 to 7, as said below
Outputs:
- new_master: float32 [48, 128, 2048], P('expert', None, 'dp')
- new_first: float32 [48, 128, 2048], P('expert', None, 'dp')
- new_second: float32 [48, 128, 2048], P('expert', None, 'dp')
- new_params: bfloat16 [48, 128, 2048], P('expert')
Inputs may be any that keep to these rules, and one draw needn't show every extreme that they name: `old_owner`: tiles are owned by devices 0 to 6 of the expert axis, exactly 4 each; the other devices own none, and their slots of the old-layout arrays are never read. `new_owner`: each device owns at most 6 tiles and some own exactly 6; the tiles of one old owner go to different new owners.
All inputs are finite; a program needn't handle non-finite values.
Results may differ from a plain program's by a relative error of at most 0.0085.
Values may be sent and summed in bfloat16 or wider, within the bound.
A program may use at most 128 MiB of HBM per device.

v0:
```python
import functools

import jax
import jax.numpy as jnp
from jax import lax
from jax.experimental import pallas as pl
from jax.experimental.pallas import tpu as pltpu
from jax.sharding import PartitionSpec as P

MESH = pl.DeviceIdType.MESH
ROWS = 16
AHEAD = 1
HOP = 1
MAIL = 2
WIDE = 2
PLAN = (1, 0)


def early(c):
    return PLAN[c % len(PLAN)] == 1


def adam_step(gradient, moment_one, moment_two, weight):
    moment_one = 0.9 * moment_one + 0.1 * gradient
    moment_two = 0.95 * moment_two + 0.05 * gradient * gradient
    update = moment_one / (1.0 - 0.9**50) / (jnp.sqrt(moment_two / (1.0 - 0.95**50)) + 1e-08)
    weight = weight - 0.05 * (update + 0.1 * weight)
    return (weight, moment_one, moment_two)


def kernel(dp, peers, owners, chunks, old_ref, new_ref, g_hbm, m_hbm, v_hbm, w_hbm, *rest):
    outs, params, rest = rest[:3], rest[3], rest[4:]
    g, state, part, up, down, stay = rest[:6]
    rest = rest[6:]
    fresh, mail, inbox, wide, wide_mail, wide_inbox = (rest[i * chunks : (i + 1) * chunks] for i in range(6))
    (in_sem, up_send, up_recv, down_send, down_recv, x_send, x_recv, w_send, w_recv,
     gu_send, gu_recv, gd_send, gd_recv) = rest[6 * chunks :]
    z = lax.axis_index("dp")
    e = lax.axis_index("expert")
    cols = stay.shape[-1]
    new_slots = params.shape[0]
    mine = pl.ds(pl.multiple_of(z * cols, cols), cols)
    owns = e < owners

    loads = [pltpu.make_async_copy(g_hbm.at[0], g, in_sem.at[0])]
    loads += [
        pltpu.make_async_copy(ref, state.at[i], in_sem.at[i + 1])
        for i, ref in enumerate((m_hbm, v_hbm, w_hbm))
    ]
    for load in loads:
        load.start()

    barrier = pltpu.get_barrier_semaphore()
    for step in range(1, peers):
        pl.semaphore_signal(
            barrier, inc=1, device_id={"expert": lax.rem(e + step, peers)}, device_id_type=MESH
        )

    @pl.when(z > 0)
    def _():
        pl.semaphore_signal(barrier, inc=1, device_id={"dp": z - 1}, device_id_type=MESH)

    @pl.when(z < dp - 1)
    def _():
        pl.semaphore_signal(barrier, inc=1, device_id={"dp": z + 1}, device_id_type=MESH)

    inner = (z > 0).astype(jnp.int32) + (z < dp - 1).astype(jnp.int32)
    pl.semaphore_wait(barrier, peers - 1 + inner)
    for load in loads:
        load.wait()

    tiles = old_ref.shape[0]
    targets = [lax.rem(e + step, peers) for step in range(peers)]

    def route(tile, carry):
        sent, taken, slots, sources = carry
        old, new = old_ref[tile], new_ref[tile]
        leaves, comes = old == e, new == e
        slots = tuple(jnp.where(leaves & (new == to), sent, slot) for to, slot in zip(targets, slots))
        sources = tuple(
            jnp.where(comes & (taken == slot), old, source) for slot, source in enumerate(sources)
        )
        return sent + leaves.astype(jnp.int32), taken + comes.astype(jnp.int32), slots, sources

    def rows(c):
        return pl.ds(c * ROWS, ROWS)

    def block(k):
        return pl.ds(k * cols, cols)

    def up_copy(c, k, raw):
        src = g.at[:, rows(c), block(k)] if raw else part.at[k, :, rows(c)]
        return pltpu.make_async_remote_copy(
            src, up.at[k, :, rows(c)], up_send.at[c, k], up_recv.at[c, k],
            device_id={"dp": z + 1}, device_id_type=MESH,
        )

    def down_copy(c, k, raw):
        src = g.at[:, rows(c), block(k)] if raw else part.at[k, :, rows(c)]
        return pltpu.make_async_remote_copy(
            src, down.at[k, :, rows(c)], down_send.at[c, k], down_recv.at[c, k],
            device_id={"dp": z - 1}, device_id_type=MESH,
        )

    def gather_copy(c, k, going_up):
        send, recv = (gu_send, gu_recv) if going_up else (gd_send, gd_recv)
        where = wide[c].at[:, :, block(k)] if early(c) else params.at[:, rows(c), block(k)]
        return pltpu.make_async_remote_copy(
            where, where, send.at[c, k], recv.at[c, k],
            device_id={"dp": z + 1 if going_up else z - 1}, device_id_type=MESH,
        )

    def mail_copy(c, to, source):
        return pltpu.make_async_remote_copy(
            mail[c].at[to], inbox[c].at[source], x_send.at[c, to], x_recv.at[c, source],
            device_id={"expert": to}, device_id_type=MESH,
        )

    def wide_copy(c, to, source):
        return pltpu.make_async_remote_copy(
            wide_mail[c].at[to], wide_inbox[c].at[source], w_send.at[c, to], w_recv.at[c, source],
            device_id={"expert": to}, device_id_type=MESH,
        )

    def first_sends(c):
        @pl.when(owns & (z == 0))
        def _():
            for k in range(dp - 1, 0, -1):
                up_copy(c, k, True).start()

        @pl.when(owns & (z == dp - 1))
        def _():
            for k in range(dp - 1):
                down_copy(c, k, True).start()

    def relay_up(c, at):
        for k in range(dp - 1, at, -1):
            up_copy(c, k, False).wait_recv()
            total = g[:, rows(c), block(k)].astype(jnp.float32) + up[k, :, rows(c)].astype(jnp.float32)
            part[k, :, rows(c)] = total.astype(jnp.bfloat16)
            up_copy(c, k, False).start()

    def relay_down(c, at):
        for k in range(at):
            down_copy(c, k, False).wait_recv()
            total = g[:, rows(c), block(k)].astype(jnp.float32) + down[k, :, rows(c)].astype(jnp.float32)
            part[k, :, rows(c)] = total.astype(jnp.bfloat16)
            down_copy(c, k, False).start()

    def relay(c, at, going_up):
        @pl.when(owns & (z == at))
        def _():
            (relay_up if going_up else relay_down)(c, at)

    def update(c):
        @pl.when(owns)
        def _():
            stay[...] = g[:, rows(c), mine].astype(jnp.float32)
            for k in range(dp):
                @pl.when(z == k)
                def _():
                    if k > 0:
                        up_copy(c, k, False).wait_recv()
                        stay[...] += up[k, :, rows(c)].astype(jnp.float32)
                    if k < dp - 1:
                        down_copy(c, k, False).wait_recv()
                        stay[...] += down[k, :, rows(c)].astype(jnp.float32)
            for slot in range(stay.shape[0]):
                values = adam_step(
                    stay[slot], state[0, slot, rows(c)], state[1, slot, rows(c)], state[2, slot, rows(c)]
                )
                values = [value.astype(jnp.bfloat16) for value in values]
                if early(c):
                    wide[c][slot, :, mine] = values.pop(0)
                for i, value in enumerate(values):
                    fresh[c][slot, i] = value
            if early(c):
                gather(c)
            for to, slot in zip(targets[1:], slots[1:]):
                mail[c][to] = fresh[c][slot]
                mail_copy(c, to, e).start()
            inbox[c][e] = fresh[c][slots[0]]

    def gather(c):
        for k in range(dp):
            @pl.when(z == k)
            def _():
                if k < dp - 1:
                    gather_copy(c, k, True).start()
                if k > 0:
                    gather_copy(c, k, False).start()

    def forward(c, hop):
        for at in range(1, dp - 1):
            @pl.when((owns & (z == at)) if early(c) else (z == at))
            def _():
                for k, going_up in ((at - hop, True), (at + hop, False)):
                    if 0 <= k < dp:
                        gather_copy(c, k, going_up).wait_recv()
                        gather_copy(c, k, going_up).start()

    def gathered(c):
        @pl.when(z == dp - 1)
        def _():
            for k in range(dp - 1):
                gather_copy(c, k, True).wait_recv()

        @pl.when(z == 0)
        def _():
            for k in range(1, dp):
                gather_copy(c, k, False).wait_recv()

    def post_wide(c):
        @pl.when(owns)
        def _():
            gathered(c)
            for to, slot in zip(targets[1:], slots[1:]):
                wide_mail[c][to] = wide[c][slot]
                wide_copy(c, to, e).start()
            wide_inbox[c][e] = wide[c][slots[0]]

    def deliver(c):
        for source in range(owners):
            @pl.when(e != source)
            def _():
                mail_copy(c, source, source).wait_recv()
                if early(c):
                    wide_copy(c, source, source).wait_recv()

        for slot in range(new_slots):
            present = taken > slot

            def kept(value):
                return jnp.where(present, value, jnp.zeros_like(value))

            if early(c):
                params[slot, rows(c)] = kept(wide_inbox[c][sources[slot]])
                outs[0][slot, rows(c)] = kept(wide_inbox[c][sources[slot], :, mine]).astype(jnp.float32)
            else:
                value = kept(inbox[c][sources[slot], 0])
                params[slot, rows(c), mine] = value
                outs[0][slot, rows(c)] = value.astype(jnp.float32)
            first = 0 if early(c) else 1
            for i in range(2):
                value = kept(inbox[c][sources[slot], first + i])
                outs[i + 1][slot, rows(c)] = value.astype(jnp.float32)
        if not early(c):
            gather(c)

    for c in range(min(AHEAD, chunks)):
        first_sends(c)
    zero = jnp.int32(0)
    _, taken, slots, sources = lax.fori_loop(
        0, tiles, route, (zero, zero, (zero,) * peers, (zero,) * new_slots)
    )
    slots = tuple(jnp.minimum(slot, stay.shape[0] - 1) for slot in slots)
    sources = tuple(jnp.minimum(source, owners - 1) for source in sources)
    jobs = []
    for c in range(chunks):
        if c >= AHEAD:
            jobs.append((c - AHEAD + 1, c, first_sends, (c,)))
        for at in range(1, dp - 1):
            jobs.append((c + at * HOP, c, relay, (c, at, True)))
            jobs.append((c + (dp - 1 - at) * HOP, c, relay, (c, at, False)))
        now = c + (dp - 1) * HOP
        jobs.append((now, c, update, (c,)))
        if not early(c):
            now += MAIL
            jobs.append((now, c, deliver, (c,)))
        for hop in range(1, dp - 1):
            jobs.append((now + hop * HOP, c, forward, (c, hop)))
        now += (dp - 1) * HOP
        if early(c):
            jobs.append((now, c, post_wide, (c,)))
            jobs.append((now + WIDE, c, deliver, (c,)))
        else:
            jobs.append((now, c, gathered, (c,)))
    for _, _, job, args in sorted(jobs, key=lambda item: item[:2]):
        job(*args)

    for c in range(chunks):
        for k in range(dp):
            reach = owns if early(c) else True

            @pl.when(reach & (z >= k) & (z < dp - 1))
            def _():
                gather_copy(c, k, True).wait_send()

            @pl.when(reach & (z <= k) & (z > 0))
            def _():
                gather_copy(c, k, False).wait_send()

        @pl.when(owns)
        def _():
            for k in range(1, dp):
                @pl.when(z < k)
                def _():
                    up_copy(c, k, False).wait_send()
            for k in range(dp - 1):
                @pl.when(z > k)
                def _():
                    down_copy(c, k, False).wait_send()
            for to in targets[1:]:
                mail_copy(c, to, e).wait_send()
                if early(c):
                    wide_copy(c, to, e).wait_send()


def shards(grad_parts, first_moment, second_moment, master_weight, old_owner, new_owner):
    dp = lax.axis_size("dp")
    peers = lax.axis_size("expert")
    old_slots, tile_rows, cols = first_moment.shape
    owners = old_owner.shape[0] // old_slots
    new_slots = min(old_slots + old_slots // 2, peers - peers // 5)
    chunks = tile_rows // ROWS
    bf16, f32 = jnp.bfloat16, jnp.float32
    dma = pltpu.SemaphoreType.DMA
    any_space = pl.BlockSpec(memory_space=pl.ANY)
    smem = pl.BlockSpec(memory_space=pltpu.SMEM)
    master = jax.ShapeDtypeStruct((new_slots, tile_rows, cols), f32)
    scratch = [
        pltpu.VMEM((old_slots, tile_rows, dp * cols), bf16),
        pltpu.VMEM((3, old_slots, tile_rows, cols), f32),
        pltpu.VMEM((dp, old_slots, tile_rows, cols), bf16),
        pltpu.VMEM((dp, old_slots, tile_rows, cols), bf16),
        pltpu.VMEM((dp, old_slots, tile_rows, cols), bf16),
        pltpu.VMEM((old_slots, ROWS, cols), f32),
    ]
    first = [early(c) for c in range(chunks)]
    kept = [2 if flag else 3 for flag in first]
    width = [dp * cols if flag else 128 for flag in first]
    span = [ROWS if flag else 16 for flag in first]
    scratch += [pltpu.VMEM((old_slots, n, ROWS, cols), bf16) for n in kept]
    scratch += [pltpu.VMEM((peers, n, ROWS, cols), bf16) for n in kept]
    scratch += [pltpu.VMEM((owners, n, ROWS, cols), bf16) for n in kept]
    scratch += [pltpu.VMEM((old_slots, r, n), bf16) for r, n in zip(span, width)]
    scratch += [pltpu.VMEM((peers, r, n), bf16) for r, n in zip(span, width)]
    scratch += [pltpu.VMEM((owners, r, n), bf16) for r, n in zip(span, width)]
    scratch += [dma((4,))] + [dma((chunks, dp))] * 4 + [dma((chunks, peers))] * 4
    scratch += [dma((chunks, dp))] * 4
    results = new_slots * tile_rows * cols * (12 + 2 * dp)
    return pl.pallas_call(
        functools.partial(kernel, dp, peers, owners, chunks),
        out_shape=(master,) * 3
        + (jax.ShapeDtypeStruct((new_slots, tile_rows, dp * cols), bf16),),
        in_specs=[smem] * 2 + [any_space] * 4,
        out_specs=(pl.BlockSpec(memory_space=pltpu.VMEM),) * 4,
        scratch_shapes=scratch,
        compiler_params=pltpu.CompilerParams(
            collective_id=0, has_side_effects=True, vmem_limit_bytes=67043328 - results - 2**19
        ),
    )(old_owner, new_owner, grad_parts, first_moment, second_moment, master_weight)


def solution(mesh):
    placed = (
        P("dp", "expert", None, None),
        P("expert", None, "dp"),
        P("expert", None, "dp"),
        P("expert", None, "dp"),
        P(),
        P(),
    )
    return jax.shard_map(
        shards,
        mesh=mesh,
        in_specs=placed,
        out_specs=(
            P("expert", None, "dp"),
            P("expert", None, "dp"),
            P("expert", None, "dp"),
            P("expert", None, None),
        ),
        check_vma=False,
    )
```

profile of v0, /device:TPU:0, one launch (start us, length us, event | category | flops | bytes accessed | tf_op | source)
XLA Modules:
  0.0 96.2 jit_solution(13051052983296230431)
XLA Ops:
  0.6 86.6 %shard_map.93 = (f32[6,128,512]{2,1,0:T(8,128)}, f32[6,128,512]{2,1,0:T(8,128)}, f32[6,128,512]{2,1,0:T(8,128)}, bf16[6,128,2048]{2,1,0:T(8,128)(2,1)}) custom-call(s32[28]{0:T(128)} %old_ref.1, s32[28]{0:T(128)} %new_ref.1, bf16[1,4,128,2048]{3,2,1,0:T(8,128)(2,1)} %g_hbm.1, f32[4,128,512]{2,1,0:T(8,128)} %m_hbm.1, f32[4,128,512]{2,1,0:T(8,128)} %v_hbm.1, ...), custom_call_target="tpu_custom_call" | custom-call | tf_op jit(solution)/shard_map/pallas_call | solution.py:342
  87.3 0.0 copy-start.2
  87.3 2.9 %copy.14 = f32[6,128,512]{2,1,0:T(8,128)} copy(f32[6,128,512]{2,1,0:T(8,128)} %get-tuple-element.8) | data formatting | bytes 3145728
  90.1 0.0 copy-done.2
  90.1 0.0 copy-start.1
  90.1 1.1 %copy.15 = f32[6,128,512]{2,1,0:T(8,128)} copy(f32[6,128,512]{2,1,0:T(8,128)S(1)} %copy-done.2) | data formatting | bytes 3145728
  91.3 0.8 copy-done.1
  92.1 0.0 copy-start
  92.1 1.1 %copy.16 = f32[6,128,512]{2,1,0:T(8,128)} copy(f32[6,128,512]{2,1,0:T(8,128)S(1)} %copy-done.1) | data formatting | bytes 3145728
  93.3 1.3 %copy-done = bf16[6,128,2048]{2,1,0:T(8,128)(2,1)S(1)} copy-done((bf16[6,128,2048]{2,1,0:T(8,128)(2,1)S(1)}, bf16[6,128,2048]{2,1,0:T(8,128)(2,1)}, u32[]{:S(2)}) %copy-start) | copy-done | bytes 3145752
  94.6 1.7 %copy.17 = bf16[6,128,2048]{2,1,0:T(8,128)(2,1)} copy(bf16[6,128,2048]{2,1,0:T(8,128)(2,1)S(1)} %copy-done) | data formatting | bytes 6291456
Async XLA Ops:
  87.3 2.9 %copy-start.2 = (f32[6,128,512]{2,1,0:T(8,128)S(1)}, f32[6,128,512]{2,1,0:T(8,128)}, u32[]{:S(2)}) copy-start(f32[6,128,512]{2,1,0:T(8,128)} %get-tuple-element.9) | copy-start | bytes 4718596
  90.1 2.0 %copy-start.1 = (f32[6,128,512]{2,1,0:T(8,128)S(1)}, f32[6,128,512]{2,1,0:T(8,128)}, u32[]{:S(2)}) copy-start(f32[6,128,512]{2,1,0:T(8,128)} %get-tuple-element.10) | copy-start | bytes 4718596
  92.1 2.5 %copy-start = (bf16[6,128,2048]{2,1,0:T(8,128)(2,1)S(1)}, bf16[6,128,2048]{2,1,0:T(8,128)(2,1)}, u32[]{:S(2)}) copy-start(bf16[6,128,2048]{2,1,0:T(8,128)(2,1)} %get-tuple-element.11) | copy-start | bytes 9437188
where the time goes:
time: 96.4 us; the launch traced here: 96.2 us
  Pallas kernels  86.6 us (90%)
  local copies, waits for them, and re-layouts  8.98 us (9%)
    pallas_call x1, Pallas kernels, shards(): pl.pallas_call(functools.partial(kernel, dp, peers, owners, chunks), out_...  86.6 us
    unnamed x10, local copies, waits for them, and re-layouts  8.98 us

commit v1 on v0

--- a/solution.py
+++ b/solution.py
@@ -29,7 +29,7 @@
 
 
 def kernel(dp, peers, owners, chunks, old_ref, new_ref, g_hbm, m_hbm, v_hbm, w_hbm, *rest):
-    outs, params, rest = rest[:3], rest[3], rest[4:]
+    moments, params, rest = rest[0], rest[1], rest[2:]
     g, state, part, up, down, stay = rest[:6]
     rest = rest[6:]
     fresh, mail, inbox, wide, wide_mail, wide_inbox = (rest[i * chunks : (i + 1) * chunks] for i in range(6))
@@ -235,15 +235,11 @@
 
             if early(c):
                 params[slot, rows(c)] = kept(wide_inbox[c][sources[slot]])
-                outs[0][slot, rows(c)] = kept(wide_inbox[c][sources[slot], :, mine]).astype(jnp.float32)
             else:
-                value = kept(inbox[c][sources[slot], 0])
-                params[slot, rows(c), mine] = value
-                outs[0][slot, rows(c)] = value.astype(jnp.float32)
+                params[slot, rows(c), mine] = kept(inbox[c][sources[slot], 0])
             first = 0 if early(c) else 1
             for i in range(2):
-                value = kept(inbox[c][sources[slot], first + i])
-                outs[i + 1][slot, rows(c)] = value.astype(jnp.float32)
+                moments[i, slot, rows(c)] = kept(inbox[c][sources[slot], first + i])
         if not early(c):
             gather(c)
 
@@ -304,6 +300,22 @@
                 mail_copy(c, to, e).wait_send()
                 if early(c):
                     wide_copy(c, to, e).wait_send()
+
+
+def widen(moments, params, w_out, m_out, v_out, p_out, staged, sems, sem):
+    new_slots, _, cols = w_out.shape
+    z = lax.axis_index("dp")
+    mine = pl.ds(pl.multiple_of(z * cols, cols), cols)
+    copies = [pltpu.make_async_copy(params, p_out, sem)]
+    copies[0].start()
+    for slot in range(new_slots):
+        parts = (params.at[slot, :, mine], moments.at[0, slot], moments.at[1, slot])
+        for i, (part, out) in enumerate(zip(parts, (w_out, m_out, v_out))):
+            staged[i, slot] = part[...].astype(jnp.float32)
+            copies.append(pltpu.make_async_copy(staged.at[i, slot], out.at[slot], sems.at[i, slot]))
+            copies[-1].start()
+    for copy in copies:
+        copy.wait()
 
 
 def shards(grad_parts, first_moment, second_moment, master_weight, old_owner, new_owner):
@@ -338,18 +350,30 @@
     scratch += [pltpu.VMEM((owners, r, n), bf16) for r, n in zip(span, width)]
     scratch += [dma((4,))] + [dma((chunks, dp))] * 4 + [dma((chunks, peers))] * 4
     scratch += [dma((chunks, dp))] * 4
-    results = new_slots * tile_rows * cols * (12 + 2 * dp)
-    return pl.pallas_call(
+    results = new_slots * tile_rows * cols * (4 + 2 * dp)
+    vmem = pl.BlockSpec(memory_space=pltpu.VMEM)
+    moments, params = pl.pallas_call(
         functools.partial(kernel, dp, peers, owners, chunks),
-        out_shape=(master,) * 3
-        + (jax.ShapeDtypeStruct((new_slots, tile_rows, dp * cols), bf16),),
+        out_shape=(
+            pltpu.VMEM((2, new_slots, tile_rows, cols), bf16),
+            pltpu.VMEM((new_slots, tile_rows, dp * cols), bf16),
+        ),
         in_specs=[smem] * 2 + [any_space] * 4,
-        out_specs=(pl.BlockSpec(memory_space=pltpu.VMEM),) * 4,
+        out_specs=(vmem,) * 2,
         scratch_shapes=scratch,
         compiler_params=pltpu.CompilerParams(
             collective_id=0, has_side_effects=True, vmem_limit_bytes=67043328 - results - 2**19
         ),
     )(old_owner, new_owner, grad_parts, first_moment, second_moment, master_weight)
+    return pl.pallas_call(
+        widen,
+        out_shape=(master,) * 3
+        + (jax.ShapeDtypeStruct((new_slots, tile_rows, dp * cols), bf16),),
+        in_specs=[vmem] * 2,
+        out_specs=(any_space,) * 4,
+        scratch_shapes=[pltpu.VMEM((3, new_slots, tile_rows, cols), f32), dma((3, new_slots)), dma],
+        compiler_params=pltpu.CompilerParams(vmem_limit_bytes=2**24),
+    )(moments, params)
 
 
 def solution(mesh):

time: 96.4 us -> 87.6 us (0.909)
  local copies, waits for them, and re-layouts: 8.98 us -> 0 us
    unnamed x10 -> x0, local copies, waits for them, and re-layouts: 8.98 us -> none
    pallas_call x0 -> x1, Pallas kernels: none -> 3.31 us  [shards(): pl.pallas_call(widen, out_shape=(master,) * 3 + (jax.ShapeDtypeStruct((ne...]
    pallas_call x1, Pallas kernels: 86.6 us -> 83.5 us  [shards(): pl.pallas_call(functools.partial(kernel, dp, peers, owners, chunks), out_...]
where the time goes in v1:
time: 87.6 us; the launch traced here: 87.5 us
  Pallas kernels  86.8 us (99%)
    pallas_call x1, Pallas kernels, shards(): pl.pallas_call(functools.partial(kernel, dp, peers, owners, chunks), out_...  83.5 us
    pallas_call x1, Pallas kernels, shards(): pl.pallas_call(widen, out_shape=(master,) * 3 + (jax.ShapeDtypeStruct((ne...  3.31 us

profile of v1, /device:TPU:0, one launch (start us, length us, event | category | flops | bytes accessed | tf_op | source)
XLA Modules:
  0.0 87.5 jit_solution(11477720886152708933)
XLA Ops:
  0.6 83.5 %shard_map.93 = (bf16[2,6,128,512]{3,2,1,0:T(8,128)(2,1)S(1)}, bf16[6,128,2048]{2,1,0:T(8,128)(2,1)S(1)}) custom-call(s32[28]{0:T(128)} %old_ref.1, s32[28]{0:T(128)} %new_ref.1, bf16[1,4,128,2048]{3,2,1,0:T(8,128)(2,1)} %g_hbm.1, f32[4,128,512]{2,1,0:T(8,128)} %m_hbm.1, f32[4,128,512]{2,1,0:T(8,128)} %v_hbm.1, f32[4,128,512]{2,1,0:T(8,128)} %w_hbm.1), custom_call_target="tpu_custom_call" | custom-call | tf_op jit(solution)/shard_map/pallas_call | solution.py:355
  84.2 3.3 %shard_map.94 = (f32[6,128,512]{2,1,0:T(8,128)}, f32[6,128,512]{2,1,0:T(8,128)}, f32[6,128,512]{2,1,0:T(8,128)}, bf16[6,128,2048]{2,1,0:T(8,128)(2,1)}) custom-call(bf16[2,6,128,512]{3,2,1,0:T(8,128)(2,1)S(1)} %get-tuple-element.6.moments, bf16[6,128,2048]{2,1,0:T(8,128)(2,1)S(1)} %get-tuple-element.7.params), custom_call_target="tpu_custom_call" | custom-call | tf_op jit(solution)/shard_map/pallas_call | solution.py:368

commit v2 on v1

v2 whole, which is shorter than its diff:
```python
import functools

import jax
import jax.numpy as jnp
from jax import lax
from jax.experimental import pallas as pl
from jax.experimental.pallas import tpu as pltpu
from jax.sharding import PartitionSpec as P

MESH = pl.DeviceIdType.MESH
ROWS = 16
PLAN = (1, 1, 0, 1, 0, 1, 0, 0)
TABLE = ((('U', 0, 3), ('U', 1, 3), ('U', 2, 3), ('U', 2, 2), ('U', 0, 2), ('U', 3, 3), ('U', 4, 3), ('U', 2, 1), ('U', 0, 1), ('U', 1, 2), ('U', 4, 2), ('X', 0, 0), ('M', 0, 0), ('X', 1, 0), ('M', 1, 0), ('X', 2, 0), ('M', 2, 0), ('U', 1, 1), ('U', 5, 3), ('U', 6, 3), ('X', 3, 0), ('M', 3, 0), ('U', 4, 1), ('X', 4, 0), ('M', 4, 0), ('U', 3, 2), ('U', 6, 2), ('V', 2, 0), ('U', 7, 3), ('W', 0, 0), ('U', 3, 1), ('U', 7, 2), ('U', 6, 1), ('V', 4, 0), ('W', 1, 0), ('X', 5, 0), ('X', 6, 0), ('U', 5, 2), ('V', 0, 0), ('M', 6, 0), ('U', 7, 1), ('U', 5, 1), ('M', 5, 0), ('V', 1, 0), ('Z', 2, 0), ('X', 7, 0), ('M', 7, 0), ('V', 6, 0), ('W', 3, 0), ('Z', 4, 0), ('V', 7, 0), ('W', 5, 0), ('V', 3, 0), ('Z', 6, 0), ('V', 5, 0), ('Z', 7, 0)), (('U', 0, 3), ('U', 1, 3), ('U', 2, 3), ('D', 0, 0), ('U', 2, 2), ('D', 1, 0), ('U', 0, 2), ('D', 2, 0), ('U', 3, 3), ('U', 4, 3), ('X', 2, 0), ('M', 2, 0), ('D', 3, 0), ('X', 0, 0), ('M', 0, 0), ('D', 4, 0), ('U', 1, 2), ('U', 4, 2), ('F', 0, 0), ('F', 0, 2), ('V', 2, 0), ('F', 1, 0), ('X', 1, 0), ('M', 1, 0), ('U', 5, 3), ('F', 0, 3), ('W', 0, 0), ('U', 6, 3), ('F', 2, 2), ('F', 3, 0), ('F', 1, 3), ('X', 4, 0), ('M', 4, 0), ('F', 1, 2), ('U', 3, 2), ('D', 5, 0), ('U', 6, 2), ('D', 6, 0), ('W', 1, 0), ('F', 2, 0), ('F', 3, 3), ('V', 0, 0), ('U', 7, 3), ('X', 3, 0), ('U', 7, 2), ('V', 4, 0), ('M', 3, 0), ('F', 2, 3), ('X', 6, 0), ('D', 7, 0), ('F', 4, 0), ('M', 6, 0), ('F', 3, 2), ('F', 5, 0), ('V', 1, 0), ('U', 5, 2), ('F', 4, 2), ('X', 7, 0), ('M', 7, 0), ('F', 4, 3), ('F', 5, 3), ('X', 5, 0), ('W', 3, 0), ('V', 6, 0), ('F', 6, 0), ('F', 5, 2), ('V', 7, 0), ('W', 5, 0), ('F', 6, 2), ('F', 6, 3), ('F', 7, 0), ('F', 7, 2), ('V', 3, 0), ('M', 5, 0), ('F', 7, 3), ('V', 5, 0)))


def EARLY(c):
    return PLAN[c] == 1


def ORDERS(dp, chunks, role):
    return TABLE[role]


def adam_step(gradient, moment_one, moment_two, weight):
    moment_one = 0.9 * moment_one + 0.1 * gradient
    moment_two = 0.95 * moment_two + 0.05 * gradient * gradient
    update = moment_one / (1.0 - 0.9**50) / (jnp.sqrt(moment_two / (1.0 - 0.95**50)) + 1e-08)
    weight = weight - 0.05 * (update + 0.1 * weight)
    return (weight, moment_one, moment_two)


def job_list(dp, chunks, role):
    jobs = []
    for c in range(chunks):
        jobs += [("U", c, k) for k in range(dp - 1, role, -1)] + [("D", c, k) for k in range(role)]
        jobs += [("X", c, 0), ("M", c, 0)]
        jobs += [("F", c, k) for k in range(role - 1, -1, -1)]
        if role > 0:
            jobs += [("F", c, k) for k in range(role + 1, dp)]
        if EARLY(c):
            jobs.append(("W", c, 0))
        jobs.append(("V", c, 0))
        if role == 0 and not EARLY(c):
            jobs.append(("Z", c, 0))
    return jobs


def kernel(dp, peers, owners, chunks, old_ref, new_ref, g_hbm, m_hbm, v_hbm, w_hbm, *rest):
    moments, params, rest = rest[0], rest[1], rest[2:]
    g, state, part, line = rest[:4]
    rest = rest[4:]
    fresh, mail, inbox, wide, wide_mail, wide_inbox = (rest[i * chunks : (i + 1) * chunks] for i in range(6))
    (g_sem, in_sem, s_send, s_recv, a_send, a_recv, x_send, x_recv, w_send, w_recv) = rest[6 * chunks :]
    z = lax.axis_index("dp")
    e = lax.axis_index("expert")
    old_slots, cols = state.shape[1], state.shape[-1]
    new_slots = params.shape[0]
    far = jnp.where(z < dp // 2, 0, 1)
    place = jnp.where(z < dp // 2, z, dp - 1 - z)
    ahead = 1 - 2 * far
    mine = pl.ds(pl.multiple_of(z * cols, cols), cols)
    owns = e < owners

    if peers & (peers - 1):
        targets = [lax.rem(e + step, peers) for step in range(peers)]
    else:
        bits = [1 << i for i in range(peers.bit_length() - 1)]
        turns = {bit: bit * (1 - 2 * lax.rem(e // bit, 2)) for bit in bits}
        targets = [e + sum(turns[bit] for bit in bits if mask & bit) for mask in (0, *range(peers - 1, 0, -1))]

    def rows(c):
        return pl.ds(c * ROWS, ROWS)

    def real(k):
        return k + far * (dp - 1 - 2 * k)

    def block(k):
        return pl.ds(pl.multiple_of(real(k) * cols, cols), cols)

    def way(right):
        return far if right else 1 - far

    def beside(right):
        return {"dp": z + ahead if right else z - ahead}

    barrier = pltpu.get_barrier_semaphore()
    for to in targets[1:]:
        pl.semaphore_signal(barrier, inc=1, device_id={"expert": to}, device_id_type=MESH)
    for step in (-1, 1):
        @pl.when((z + step >= 0) & (z + step < dp))
        def _():
            pl.semaphore_signal(barrier, inc=1, device_id={"dp": z + step}, device_id_type=MESH)

    g_loads = [
        pltpu.make_async_copy(g_hbm.at[0, :, rows(c)], g.at[:, rows(c)], g_sem.at[c]) for c in range(chunks)
    ]
    loads = [
        pltpu.make_async_copy(ref, state.at[i], in_sem.at[i]) for i, ref in enumerate((m_hbm, v_hbm, w_hbm))
    ]

    @pl.when(owns)
    def _():
        for load in g_loads[:1] + loads + g_loads[1:]:
            load.start()

    inner = (z > 0).astype(jnp.int32) + (z < dp - 1).astype(jnp.int32)
    pl.semaphore_wait(barrier, peers - 1 + inner)

    def route(tile, carry):
        sent, taken, slots, sources = carry
        old, new = old_ref[tile], new_ref[tile]
        leaves, comes = old == e, new == e
        slots = tuple(jnp.where(leaves & (new == to), sent, slot) for to, slot in zip(targets, slots))
        sources = tuple(
            jnp.where(comes & (taken == slot), old, source) for slot, source in enumerate(sources)
        )
        return sent + leaves.astype(jnp.int32), taken + comes.astype(jnp.int32), slots, sources

    def sum_copy(c, k, right, raw=False):
        src = g.at[:, rows(c), block(k)] if raw else part.at[real(k), :, rows(c)]
        at = (way(right), c, real(k))
        return pltpu.make_async_remote_copy(
            src, line.at[way(right), real(k), :, rows(c)], s_send.at[at], s_recv.at[at],
            device_id=beside(right), device_id_type=MESH,
        )

    def gather_copy(c, k, right):
        where = wide[c].at[:, :, block(k)] if EARLY(c) else params.at[:, rows(c), block(k)]
        at = (way(right), c, real(k))
        return pltpu.make_async_remote_copy(
            where, where, a_send.at[at], a_recv.at[at], device_id=beside(right), device_id_type=MESH,
        )

    def mail_copy(c, to, source):
        return pltpu.make_async_remote_copy(
            mail[c].at[to], inbox[c].at[source], x_send.at[c, to], x_recv.at[c, source],
            device_id={"expert": to}, device_id_type=MESH,
        )

    def wide_copy(c, to, source):
        return pltpu.make_async_remote_copy(
            wide_mail[c].at[to], wide_inbox[c].at[source], w_send.at[c, to], w_recv.at[c, source],
            device_id={"expert": to}, device_id_type=MESH,
        )

    def arrived(c, k, right):
        return line[way(right), real(k), :, rows(c)].astype(jnp.float32)

    def add_and_send(c, k, right):
        sum_copy(c, k, right).wait_recv()
        total = g[:, rows(c), block(k)].astype(jnp.float32) + arrived(c, k, right)
        part[real(k), :, rows(c)] = total.astype(jnp.bfloat16)
        sum_copy(c, k, right).start()

    def gather(c, role):
        gather_copy(c, role, True).start()
        if role > 0:
            gather_copy(c, role, False).start()

    def update(c, role):
        sides = [right for right in (True, False) if role > 0 or not right]
        for right in sides:
            sum_copy(c, role, right).wait_recv()
        for slot in range(old_slots):
            gradient = g[slot, rows(c), mine].astype(jnp.float32)
            for right in sides:
                gradient += line[way(right), z, slot, rows(c)].astype(jnp.float32)
            values = adam_step(
                gradient, state[0, slot, rows(c)], state[1, slot, rows(c)], state[2, slot, rows(c)]
            )
            values = [value.astype(jnp.bfloat16) for value in values]
            if EARLY(c):
                wide[c][slot, :, mine] = values.pop(0)
            for i, value in enumerate(values):
                fresh[c][slot, i] = value
        if EARLY(c):
            gather(c, role)

    def post(c, slots):
        for to, slot in zip(targets[1:], slots[1:]):
            mail[c][to] = fresh[c][slot]
            mail_copy(c, to, e).start()
        inbox[c][e] = fresh[c][slots[0]]

    def last_arrivals(c, role):
        if role == 0:
            for k in range(1, dp):
                gather_copy(c, k, False).wait_recv()

    def post_wide(c, role, slots):
        last_arrivals(c, role)
        for to, slot in zip(targets[1:], slots[1:]):
            wide_mail[c][to] = wide[c][slot]
            wide_copy(c, to, e).start()
        wide_inbox[c][e] = wide[c][slots[0]]

    def deliver(c, role, taken, sources):
        for source in range(owners):
            @pl.when(e != source)
            def _():
                mail_copy(c, source, source).wait_recv()
                if EARLY(c):
                    wide_copy(c, source, source).wait_recv()

        for slot in range(new_slots):
            present = taken > slot

            def kept(value):
                return jnp.where(present, value, jnp.zeros_like(value))

            if EARLY(c):
                params[slot, rows(c)] = kept(wide_inbox[c][sources[slot]])
            else:
                params[slot, rows(c), mine] = kept(inbox[c][sources[slot], 0])
            first = 0 if EARLY(c) else 1
            for i in range(2):
                moments[i, slot, rows(c)] = kept(inbox[c][sources[slot], first + i])
        if not EARLY(c):
            gather(c, role)

    def run(role, order, slots, taken, sources, loaded):
        for kind, c, k in order:
            by_owners = kind in "UDXM" or (kind in "FW" and EARLY(c))

            def job():
                if kind in "UDX" and c not in loaded:
                    loaded.append(c)
                    g_loads[c].wait()
                if kind == "X" and "state" not in loaded:
                    loaded.append("state")
                    for load in loads:
                        load.wait()
                if kind == "U" and role == 0:
                    sum_copy(c, k, True, True).start()
                elif kind in "UD":
                    add_and_send(c, k, kind == "U")
                elif kind == "X":
                    update(c, role)
                elif kind == "M":
                    post(c, slots)
                elif kind == "F":
                    gather_copy(c, k, k < role).wait_recv()
                    gather_copy(c, k, k < role).start()
                elif kind == "W":
                    post_wide(c, role, slots)
                elif kind == "V":
                    deliver(c, role, taken, sources)
                else:
                    last_arrivals(c, role)

            if by_owners:
                pl.when(owns)(job)
            else:
                job()

    orders = [ORDERS(dp, chunks, role) for role in range(dp // 2)]
    lead = 0
    while orders[0][lead][:2] == ("U", 0):
        lead += 1
    loaded = [[] for _ in orders]

    @pl.when(place == 0)
    def _():
        run(0, orders[0][:lead], None, None, None, loaded[0])

    zero = jnp.int32(0)
    _, taken, slots, sources = lax.fori_loop(
        0, old_ref.shape[0], route, (zero, zero, (zero,) * peers, (zero,) * new_slots)
    )
    slots = tuple(jnp.minimum(slot, old_slots - 1) for slot in slots)
    sources = tuple(jnp.minimum(source, owners - 1) for source in sources)

    for role, order in enumerate(orders):
        @pl.when(place == role)
        def _():
            run(role, order[lead:] if role == 0 else order, slots, taken, sources, loaded[role])

            def gathers_sent(c):
                for k in range(dp):
                    if k <= role:
                        gather_copy(c, k, True).wait_send()
                    if k >= role > 0:
                        gather_copy(c, k, False).wait_send()

            for c in range(chunks):
                if not EARLY(c):
                    gathers_sent(c)

            @pl.when(owns)
            def _():
                for c in range(chunks):
                    if EARLY(c):
                        gathers_sent(c)
                    for k in range(dp):
                        if k != role:
                            sum_copy(c, k, k > role).wait_send()

    @pl.when(owns)
    def _():
        for c in range(chunks):
            for to in targets[1:]:
                mail_copy(c, to, e).wait_send()
                if EARLY(c):
                    wide_copy(c, to, e).wait_send()


def widen(moments, params, w_out, m_out, v_out, p_out, staged, sems, sem):
    new_slots, _, cols = w_out.shape
    z = lax.axis_index("dp")
    mine = pl.ds(pl.multiple_of(z * cols, cols), cols)
    copies = [pltpu.make_async_copy(params, p_out, sem)]
    copies[0].start()
    for slot in range(new_slots):
        parts = (params.at[slot, :, mine], moments.at[0, slot], moments.at[1, slot])
        for i, (part, out) in enumerate(zip(parts, (w_out, m_out, v_out))):
            staged[i, slot] = part[...].astype(jnp.float32)
            copies.append(pltpu.make_async_copy(staged.at[i, slot], out.at[slot], sems.at[i, slot]))
            copies[-1].start()
    for copy in copies:
        copy.wait()


def shards(grad_parts, first_moment, second_moment, master_weight, old_owner, new_owner):
    dp = lax.axis_size("dp")
    peers = lax.axis_size("expert")
    old_slots, tile_rows, cols = first_moment.shape
    owners = old_owner.shape[0] // old_slots
    new_slots = min(old_slots + old_slots // 2, peers - peers // 5)
    chunks = tile_rows // ROWS
    bf16, f32 = jnp.bfloat16, jnp.float32
    dma = pltpu.SemaphoreType.DMA
    any_space = pl.BlockSpec(memory_space=pl.ANY)
    smem = pl.BlockSpec(memory_space=pltpu.SMEM)
    vmem = pl.BlockSpec(memory_space=pltpu.VMEM)
    master = jax.ShapeDtypeStruct((new_slots, tile_rows, cols), f32)
    scratch = [
        pltpu.VMEM((old_slots, tile_rows, dp * cols), bf16),
        pltpu.VMEM((3, old_slots, tile_rows, cols), f32),
        pltpu.VMEM((dp, old_slots, tile_rows, cols), bf16),
        pltpu.VMEM((2, dp, old_slots, tile_rows, cols), bf16),
    ]
    first = [EARLY(c) for c in range(chunks)]
    kept = [2 if flag else 3 for flag in first]
    width = [dp * cols if flag else 128 for flag in first]
    scratch += [pltpu.VMEM((old_slots, n, ROWS, cols), bf16) for n in kept]
    scratch += [pltpu.VMEM((peers, n, ROWS, cols), bf16) for n in kept]
    scratch += [pltpu.VMEM((owners, n, ROWS, cols), bf16) for n in kept]
    scratch += [pltpu.VMEM((old_slots, ROWS, n), bf16) for n in width]
    scratch += [pltpu.VMEM((peers, ROWS, n), bf16) for n in width]
    scratch += [pltpu.VMEM((owners, ROWS, n), bf16) for n in width]
    scratch += [dma((chunks,)), dma((3,))] + [dma((2, chunks, dp))] * 4 + [dma((chunks, peers))] * 4
    results = new_slots * tile_rows * cols * (4 + 2 * dp)
    moments, params = pl.pallas_call(
        functools.partial(kernel, dp, peers, owners, chunks),
        out_shape=(
            pltpu.VMEM((2, new_slots, tile_rows, cols), bf16),
            pltpu.VMEM((new_slots, tile_rows, dp * cols), bf16),
        ),
        in_specs=[smem] * 2 + [any_space] * 4,
        out_specs=(vmem,) * 2,
        scratch_shapes=scratch,
        compiler_params=pltpu.CompilerParams(
            collective_id=0, has_side_effects=True, vmem_limit_bytes=67043328 - results - 2**19
        ),
    )(old_owner, new_owner, grad_parts, first_moment, second_moment, master_weight)
    return pl.pallas_call(
        widen,
        out_shape=(master,) * 3
        + (jax.ShapeDtypeStruct((new_slots, tile_rows, dp * cols), bf16),),
        in_specs=[vmem] * 2,
        out_specs=(any_space,) * 4,
        scratch_shapes=[pltpu.VMEM((3, new_slots, tile_rows, cols), f32), dma((3, new_slots)), dma],
        compiler_params=pltpu.CompilerParams(vmem_limit_bytes=2**24),
    )(moments, params)


def solution(mesh):
    placed = (
        P("dp", "expert", None, None),
        P("expert", None, "dp"),
        P("expert", None, "dp"),
        P("expert", None, "dp"),
        P(),
        P(),
    )
    return jax.shard_map(
        shards,
        mesh=mesh,
        in_specs=placed,
        out_specs=(
            P("expert", None, "dp"),
            P("expert", None, "dp"),
            P("expert", None, "dp"),
            P("expert", None, None),
        ),
        check_vma=False,
    )
```

time: 87.6 us -> 81.1 us (0.926)
  Pallas kernels: 86.8 us -> 80.3 us
    pallas_call x1, Pallas kernels: 83.5 us -> 77 us  [shards(): pl.pallas_call(functools.partial(kernel, dp, peers, owners, chunks), out_...]
where the time goes in v2:
time: 81.1 us; the launch traced here: 80.9 us
  Pallas kernels  80.3 us (99%)
    pallas_call x1, Pallas kernels, shards(): pl.pallas_call(functools.partial(kernel, dp, peers, owners, chunks), out_...  77 us
    pallas_call x1, Pallas kernels, shards(): pl.pallas_call(widen, out_shape=(master,) * 3 + (jax.ShapeDtypeStruct((ne...  3.31 us

profile of v2, /device:TPU:0, one launch (start us, length us, event | category | flops | bytes accessed | tf_op | source)
XLA Modules:
  0.0 80.9 jit_solution(7078967073837233884)
XLA Ops:
  0.6 77.0 %shard_map.93 = (bf16[2,6,128,512]{3,2,1,0:T(8,128)(2,1)S(1)}, bf16[6,128,2048]{2,1,0:T(8,128)(2,1)S(1)}) custom-call(s32[28]{0:T(128)} %old_ref.1, s32[28]{0:T(128)} %new_ref.1, bf16[1,4,128,2048]{3,2,1,0:T(8,128)(2,1)} %g_hbm.1, f32[4,128,512]{2,1,0:T(8,128)} %m_hbm.1, f32[4,128,512]{2,1,0:T(8,128)} %v_hbm.1, f32[4,128,512]{2,1,0:T(8,128)} %w_hbm.1), custom_call_target="tpu_custom_call" | custom-call | tf_op jit(solution)/shard_map/pallas_call | solution.py:353
  77.6 3.3 %shard_map.94 = (f32[6,128,512]{2,1,0:T(8,128)}, f32[6,128,512]{2,1,0:T(8,128)}, f32[6,128,512]{2,1,0:T(8,128)}, bf16[6,128,2048]{2,1,0:T(8,128)(2,1)}) custom-call(bf16[2,6,128,512]{3,2,1,0:T(8,128)(2,1)S(1)} %get-tuple-element.6.moments, bf16[6,128,2048]{2,1,0:T(8,128)(2,1)S(1)} %get-tuple-element.7.params), custom_call_target="tpu_custom_call" | custom-call | tf_op jit(solution)/shard_map/pallas_call | solution.py:366

commit v3 on v2

v3 whole, which is shorter than its diff:
```python
import functools
import typing

import jax
import jax.numpy as jnp
from jax import lax
from jax.experimental import pallas as pl
from jax.experimental.pallas import tpu as pltpu
from jax.sharding import PartitionSpec as P

MESH = pl.DeviceIdType.MESH
ROWS = 16
KINDS = 'UDXMWFVZ'
PARTS = (1, 1, 1, 1, 1, 1, 1, 1)
EARLY = (0, 1, 1, 1, 0, 1, 0, 0)
SPLIT = (1, 0, 0, 0, 0, 0, 0, 1)
ORDERS = (
    (
        13, 43, 2, 3, 23, 1, 12, 33, 42, 11, 2010, 41, 63, 62, 53, 3010, 73, 2040, 61, 3040, 2000, 22, 52, 2020,
        21, 3020, 51, 32, 4000, 72, 2030, 3000, 3030, 4010, 2060, 3060, 2050, 71, 3050, 2070, 4070, 31, 6000,
        6040, 6060, 4020, 6010, 6070, 4050, 4030, 6020, 3070, 6050, 6030, 7040, 7000, 7070, 7060,
    ),
    (
        13, 43, 2, 1010, 3, 23, 1040, 2000, 4000, 12, 1000, 33, 1020, 3000, 42, 6000, 2010, 3010, 1030, 5010,
        2040, 3040, 63, 5002, 62, 5012, 53, 5013, 4010, 73, 7000, 1060, 6040, 2060, 22, 1050, 52, 1070, 3060,
        5020, 5042, 2020, 3020, 2050, 3050, 32, 72, 5023, 5022, 4020, 5052, 5050, 6060, 2070, 5030, 2030, 4070,
        3070, 3030, 5053, 5000, 5062, 5033, 5040, 5032, 4030, 6070, 6010, 5070, 7070, 5043, 6020, 5060, 5072,
        4050, 5073, 5003, 5063, 6030, 6050,
    ),
)


def adam_step(gradient, moment_one, moment_two, weight):
    moment_one = 0.9 * moment_one + 0.1 * gradient
    moment_two = 0.95 * moment_two + 0.05 * gradient * gradient
    update = moment_one / (1.0 - 0.9**50) / (jnp.sqrt(moment_two / (1.0 - 0.95**50)) + 1e-08)
    weight = weight - 0.05 * (update + 0.1 * weight)
    return (weight, moment_one, moment_two)


class Chunk(typing.NamedTuple):
    row: int
    col: int
    width: int
    early: bool
    split: bool


def job_list(dp, chunks, role):
    jobs = []
    for c, chunk in enumerate(chunks):
        jobs += [("U", c, k) for k in range(dp - 1, role, -1)] + [("D", c, k) for k in range(role)] + [("X", c, 0)]
        passed = [("F", c, k) for k in range(role - 1, -1, -1)]
        if role > 0:
            passed += [("F", c, k) for k in range(role + 1, dp)]
        if chunk.early:
            jobs += [("M", c, 0)] + passed + [("W", c, 0), ("V", c, 0)]
        else:
            jobs += [("W", c, 0)] * chunk.split + [("M", c, 0), ("V", c, 0)] + passed
            jobs += [("Z", c, 0)] * (chunk.split or role == 0)
    return jobs


def plan(dp, tile_rows, cols):
    tuned = (dp == len(ORDERS) * 2) and tile_rows == ROWS * len(PARTS) and cols % (128 * max(PARTS)) == 0
    parts = PARTS if tuned else (1,) * (tile_rows // ROWS)
    spans = [(i * ROWS, j * (cols // n), cols // n) for i, n in enumerate(parts) for j in range(n)]
    chunks = [
        Chunk(*span, *((EARLY[c] == 1, SPLIT[c] == 1) if tuned else (c % 2 == 0, False)))
        for c, span in enumerate(spans)
    ]
    orders = [job_list(dp, chunks, role) for role in range(dp // 2)]
    if tuned:
        orders = [
            [(KINDS[code // 1000], code // 10 % 100, code % 10) for code in coded] for coded in ORDERS
        ]
    return chunks, orders


def kernel(dp, peers, owners, chunks, orders, old_ref, new_ref, g_hbm, m_hbm, v_hbm, w_hbm, *rest):
    moments, params, rest = rest[0], rest[1], rest[2:]
    g, state, part, line = rest[:4]
    rest = rest[4:]
    count = len(chunks)
    fresh, mail, inbox, wide, wide_mail, wide_inbox = (rest[i * count : (i + 1) * count] for i in range(6))
    (g_sem, in_sem, s_send, s_recv, a_send, a_recv, x_send, x_recv, w_send, w_recv) = rest[6 * count :]
    z = lax.axis_index("dp")
    e = lax.axis_index("expert")
    old_slots, cols = state.shape[1], state.shape[-1]
    new_slots = params.shape[0]
    far = jnp.where(z < dp // 2, 0, 1)
    place = jnp.where(z < dp // 2, z, dp - 1 - z)
    ahead = 1 - 2 * far
    owns = e < owners

    if peers & (peers - 1):
        targets = [lax.rem(e + step, peers) for step in range(peers)]
    else:
        bits = [1 << i for i in range(peers.bit_length() - 1)]
        turns = {bit: bit * (1 - 2 * lax.rem(e // bit, 2)) for bit in bits}
        targets = [e + sum(turns[bit] for bit in bits if mask & bit) for mask in (0, *range(peers - 1, 0, -1))]

    def rows(c):
        return pl.ds(chunks[c].row, ROWS)

    def span(c):
        return pl.ds(chunks[c].col, chunks[c].width)

    def real(k):
        return k + far * (dp - 1 - 2 * k)

    def block(c, k):
        return pl.ds(pl.multiple_of(real(k) * cols + chunks[c].col, 128), chunks[c].width)

    def wide_block(c, k):
        return pl.ds(pl.multiple_of(k * chunks[c].width, 128), chunks[c].width)

    def mine(c):
        return pl.ds(pl.multiple_of(z * cols + chunks[c].col, 128), chunks[c].width)

    def way(right):
        return far if right else 1 - far

    def beside(right):
        return {"dp": z + ahead if right else z - ahead}

    barrier = pltpu.get_barrier_semaphore()
    for to in targets[1:]:
        pl.semaphore_signal(barrier, inc=1, device_id={"expert": to}, device_id_type=MESH)
    for step in (-1, 1):
        @pl.when((z + step >= 0) & (z + step < dp))
        def _():
            pl.semaphore_signal(barrier, inc=1, device_id={"dp": z + step}, device_id_type=MESH)

    g_loads = [
        pltpu.make_async_copy(g_hbm.at[0, :, pl.ds(row, ROWS)], g.at[:, pl.ds(row, ROWS)], g_sem.at[row // ROWS])
        for row in range(0, g.shape[1], ROWS)
    ]
    loads = [
        pltpu.make_async_copy(ref, state.at[i], in_sem) for i, ref in enumerate((m_hbm, v_hbm, w_hbm))
    ]

    @pl.when(owns)
    def _():
        for load in g_loads[:1] + loads + g_loads[1:]:
            load.start()

    inner = (z > 0).astype(jnp.int32) + (z < dp - 1).astype(jnp.int32)
    pl.semaphore_wait(barrier, peers - 1 + inner)

    def route(tile, carry):
        sent, taken, slots, sources = carry
        old, new = old_ref[tile], new_ref[tile]
        leaves, comes = old == e, new == e
        slots = tuple(jnp.where(leaves & (new == to), sent, slot) for to, slot in zip(targets, slots))
        sources = tuple(
            jnp.where(comes & (taken == slot), old, source) for slot, source in enumerate(sources)
        )
        return sent + leaves.astype(jnp.int32), taken + comes.astype(jnp.int32), slots, sources

    def taken_by(sem, ref):
        pltpu.make_async_copy(ref, ref, sem).wait()

    def sum_copy(c, k, right, raw=False):
        src = g.at[:, rows(c), block(c, k)] if raw else part.at[real(k), :, rows(c), span(c)]
        return pltpu.make_async_remote_copy(
            src, line.at[way(right), real(k), :, rows(c), span(c)], s_send, s_recv.at[c, real(k)],
            device_id=beside(right), device_id_type=MESH,
        )

    def gather_copy(c, k, right, to_end):
        where = wide[c].at[:, :, wide_block(c, real(k))] if chunks[c].early else params.at[:, rows(c), block(c, k)]
        return pltpu.make_async_remote_copy(
            where, where, a_send.at[c], a_recv.at[c, real(0 if to_end else k)],
            device_id=beside(right), device_id_type=MESH,
        )

    def gather_send(c, k, right, role):
        gather_copy(c, k, right, role == 1 and not right).start()

    def gather_bytes(c, pieces):
        ref = g if chunks[c].early else params
        return ref.at[:, pl.ds(0, pieces * ROWS), pl.ds(0, chunks[c].width)]

    def mail_copy(c, to):
        return pltpu.make_async_remote_copy(
            mail[c].at[to], inbox[c].at[e], x_send.at[c], x_recv.at[c],
            device_id={"expert": to}, device_id_type=MESH,
        )

    def mail_bytes(c, boxes):
        return mail[c].at[pl.ds(0, boxes)]

    def weights_copy(c, to):
        return pltpu.make_async_remote_copy(
            wide_mail[c].at[to], wide_inbox[c].at[e], w_send.at[c], w_recv.at[c],
            device_id={"expert": to}, device_id_type=MESH,
        )

    def weights_bytes(c, boxes):
        return wide_mail[c].at[pl.ds(0, boxes)]

    def arrived(c, k, right):
        return line[way(right), real(k), :, rows(c), span(c)].astype(jnp.float32)

    def add_and_send(c, k, right):
        sum_copy(c, k, right).wait_recv()
        total = g[:, rows(c), block(c, k)].astype(jnp.float32) + arrived(c, k, right)
        part[real(k), :, rows(c), span(c)] = total.astype(jnp.bfloat16)
        sum_copy(c, k, right).start()

    def gather(c, role):
        gather_send(c, role, True, role)
        if role > 0:
            gather_send(c, role, False, role)

    def update(c, role):
        sides = [right for right in (True, False) if role > 0 or not right]
        at = line.at[pl.ds(0, len(sides)), z, :, rows(c), span(c)]
        taken_by(s_recv.at[c, z], at)
        for slot in range(old_slots):
            gradient = g[slot, rows(c), mine(c)].astype(jnp.float32)
            for right in sides:
                gradient += line[way(right), z, slot, rows(c), span(c)].astype(jnp.float32)
            values = adam_step(gradient, *(state[i, slot, rows(c), span(c)] for i in range(3)))
            values = [value.astype(jnp.bfloat16) for value in values]
            if chunks[c].early:
                wide[c][slot, :, wide_block(c, z)] = values.pop(0)
            elif chunks[c].split:
                wide[c][slot] = values.pop(0)
            for i, value in enumerate(values):
                fresh[c][slot, i] = value
        if chunks[c].early:
            gather(c, role)

    def post(c, slots):
        for to, slot in zip(targets[1:], slots[1:]):
            mail[c][to] = fresh[c][slot]
            mail_copy(c, to).start()
        inbox[c][e] = fresh[c][slots[0]]

    def last_arrivals(c, role):
        if role == 0:
            taken_by(a_recv.at[c, z], gather_bytes(c, dp - 1))

    def post_weights(c, role, slots):
        if chunks[c].early:
            last_arrivals(c, role)
        for to, slot in zip(targets[1:], slots[1:]):
            wide_mail[c][to] = wide[c][slot]
            weights_copy(c, to).start()
        wide_inbox[c][e] = wide[c][slots[0]]

    def receive(c, moments_too, weights_too):
        for mask, boxes in ((owns, owners - 1), (e >= owners, owners)):
            @pl.when(mask)
            def _():
                if moments_too:
                    taken_by(x_recv.at[c], mail_bytes(c, boxes))
                if weights_too:
                    taken_by(w_recv.at[c], weights_bytes(c, boxes))

    def kept(slot, taken, value):
        return jnp.where(taken > slot, value, jnp.zeros_like(value))

    def place_moments(c, taken, sources):
        first = inbox[c].shape[1] - 2
        for slot in range(new_slots):
            for i in range(2):
                moments[i, slot, rows(c), span(c)] = kept(slot, taken, inbox[c][sources[slot], first + i])

    def deliver(c, role, taken, sources):
        receive(c, not chunks[c].split, chunks[c].early or chunks[c].split)
        for slot in range(new_slots):
            if chunks[c].early:
                for k in range(dp):
                    value = wide_inbox[c][sources[slot], :, wide_block(c, k)]
                    params[slot, rows(c), pl.ds(k * cols + chunks[c].col, chunks[c].width)] = kept(slot, taken, value)
            else:
                box = wide_inbox[c][sources[slot]] if chunks[c].split else inbox[c][sources[slot], 0]
                params[slot, rows(c), mine(c)] = kept(slot, taken, box)
        if not chunks[c].early:
            gather(c, role)
        if not chunks[c].split:
            place_moments(c, taken, sources)

    def finish(c, role, taken, sources):
        if chunks[c].split:
            receive(c, True, False)
            place_moments(c, taken, sources)
        last_arrivals(c, role)

    def run(role, order, slots, taken, sources, loaded):
        for kind, c, k in order:
            by_owners = kind in "UDXMW" or (kind == "F" and chunks[c].early)

            def job():
                if kind in "UDX" and chunks[c].row not in loaded:
                    loaded.append(chunks[c].row)
                    g_loads[chunks[c].row // ROWS].wait()
                if kind == "X" and -1 not in loaded:
                    loaded.append(-1)
                    taken_by(in_sem, state)
                if kind == "U" and role == 0:
                    sum_copy(c, k, True, True).start()
                elif kind in "UD":
                    add_and_send(c, k, kind == "U")
                elif kind == "X":
                    update(c, role)
                elif kind == "M":
                    post(c, slots)
                elif kind == "F":
                    gather_copy(c, k, k < role, False).wait_recv()
                    gather_send(c, k, k < role, role)
                elif kind == "W":
                    post_weights(c, role, slots)
                elif kind == "V":
                    deliver(c, role, taken, sources)
                else:
                    finish(c, role, taken, sources)

            if by_owners:
                pl.when(owns)(job)
            else:
                job()

    lead = 0
    while orders[0][lead][:2] == ("U", 0):
        lead += 1
    loaded = [[] for _ in orders]

    @pl.when(place == 0)
    def _():
        run(0, orders[0][:lead], None, None, None, loaded[0])

    zero = jnp.int32(0)
    _, taken, slots, sources = lax.fori_loop(
        0, old_ref.shape[0], route, (zero, zero, (zero,) * peers, (zero,) * new_slots)
    )
    slots = tuple(jnp.minimum(slot, old_slots - 1) for slot in slots)
    sources = tuple(jnp.minimum(source, owners - 1) for source in sources)

    for role, order in enumerate(orders):
        @pl.when(place == role)
        def _():
            run(role, order[lead:] if role == 0 else order, slots, taken, sources, loaded[role])

            def gathers_sent(c):
                taken_by(a_send.at[c], gather_bytes(c, dp + 1 if role > 0 else 1))

            for c in range(count):
                if not chunks[c].early:
                    gathers_sent(c)

            @pl.when(owns)
            def _():
                for c in range(count):
                    if chunks[c].early:
                        gathers_sent(c)

    @pl.when(owns)
    def _():
        taken_by(s_send, part.at[pl.ds(0, dp - 1)])
        for c in range(count):
            taken_by(x_send.at[c], mail_bytes(c, peers - 1))
            if chunks[c].early or chunks[c].split:
                taken_by(w_send.at[c], weights_bytes(c, peers - 1))


def widen(moments, params, w_out, m_out, v_out, p_out, staged, sems, sem):
    new_slots, _, cols = w_out.shape
    z = lax.axis_index("dp")
    mine = pl.ds(pl.multiple_of(z * cols, cols), cols)
    copies = [pltpu.make_async_copy(params, p_out, sem)]
    copies[0].start()
    for slot in range(new_slots):
        parts = (params.at[slot, :, mine], moments.at[0, slot], moments.at[1, slot])
        for i, (part, out) in enumerate(zip(parts, (w_out, m_out, v_out))):
            staged[i, slot] = part[...].astype(jnp.float32)
            copies.append(pltpu.make_async_copy(staged.at[i, slot], out.at[slot], sems.at[i, slot]))
            copies[-1].start()
    for copy in copies:
        copy.wait()


def shards(grad_parts, first_moment, second_moment, master_weight, old_owner, new_owner):
    dp = lax.axis_size("dp")
    peers = lax.axis_size("expert")
    old_slots, tile_rows, cols = first_moment.shape
    owners = old_owner.shape[0] // old_slots
    new_slots = min(old_slots + old_slots // 2, peers - peers // 5)
    chunks, orders = plan(dp, tile_rows, cols)
    count = len(chunks)
    bf16, f32 = jnp.bfloat16, jnp.float32
    dma = pltpu.SemaphoreType.DMA
    any_space = pl.BlockSpec(memory_space=pl.ANY)
    smem = pl.BlockSpec(memory_space=pltpu.SMEM)
    vmem = pl.BlockSpec(memory_space=pltpu.VMEM)
    master = jax.ShapeDtypeStruct((new_slots, tile_rows, cols), f32)
    scratch = [
        pltpu.VMEM((old_slots, tile_rows, dp * cols), bf16),
        pltpu.VMEM((3, old_slots, tile_rows, cols), f32),
        pltpu.VMEM((dp, old_slots, tile_rows, cols), bf16),
        pltpu.VMEM((2, dp, old_slots, tile_rows, cols), bf16),
    ]
    kept = [2 if chunk.early or chunk.split else 3 for chunk in chunks]
    wide = [chunk.width * (dp if chunk.early else 1) if chunk.early or chunk.split else 128 for chunk in chunks]
    for boxes in (old_slots, peers, owners):
        scratch += [pltpu.VMEM((boxes, n, ROWS, chunk.width), bf16) for n, chunk in zip(kept, chunks)]
    for boxes in (old_slots, peers, owners):
        scratch += [pltpu.VMEM((boxes, ROWS, n), bf16) for n in wide]
    scratch += [dma((tile_rows // ROWS,)), dma, dma] + [dma((count, dp)), dma((count,)), dma((count, dp))]
    scratch += [dma((count,))] * 4
    results = new_slots * tile_rows * cols * (4 + 2 * dp)
    moments, params = pl.pallas_call(
        functools.partial(kernel, dp, peers, owners, chunks, orders),
        out_shape=(
            pltpu.VMEM((2, new_slots, tile_rows, cols), bf16),
            pltpu.VMEM((new_slots, tile_rows, dp * cols), bf16),
        ),
        in_specs=[smem] * 2 + [any_space] * 4,
        out_specs=(vmem,) * 2,
        scratch_shapes=scratch,
        compiler_params=pltpu.CompilerParams(
            collective_id=0, has_side_effects=True, vmem_limit_bytes=67043328 - results - 2**19
        ),
    )(old_owner, new_owner, grad_parts, first_moment, second_moment, master_weight)
    return pl.pallas_call(
        widen,
        out_shape=(master,) * 3
        + (jax.ShapeDtypeStruct((new_slots, tile_rows, dp * cols), bf16),),
        in_specs=[vmem] * 2,
        out_specs=(any_space,) * 4,
        scratch_shapes=[pltpu.VMEM((3, new_slots, tile_rows, cols), f32), dma((3, new_slots)), dma],
        compiler_params=pltpu.CompilerParams(vmem_limit_bytes=2**24),
    )(moments, params)


def solution(mesh):
    placed = (
        P("dp", "expert", None, None),
        P("expert", None, "dp"),
        P("expert", None, "dp"),
        P("expert", None, "dp"),
        P(),
        P(),
    )
    return jax.shard_map(
        shards,
        mesh=mesh,
        in_specs=placed,
        out_specs=(
            P("expert", None, "dp"),
            P("expert", None, "dp"),
            P("expert", None, "dp"),
            P("expert", None, None),
        ),
        check_vma=False,
    )
```

time: 81.1 us -> 76.4 us (0.942)
  Pallas kernels: 80.3 us -> 75.6 us
    pallas_call x1, Pallas kernels: 77 us -> 72.3 us  [shards(): pl.pallas_call(functools.partial(kernel, dp, peers, owners, chunks, order...]
where the time goes in v3:
time: 76.4 us; the launch traced here: 76.2 us
  Pallas kernels  75.6 us (99%)
    pallas_call x1, Pallas kernels, shards(): pl.pallas_call(functools.partial(kernel, dp, peers, owners, chunks, order...  72.3 us
    pallas_call x1, Pallas kernels, shards(): pl.pallas_call(widen, out_shape=(master,) * 3 + (jax.ShapeDtypeStruct((ne...  3.31 us

profile of v3, /device:TPU:0, one launch (start us, length us, event | category | flops | bytes accessed | tf_op | source)
XLA Modules:
  0.0 76.2 jit_solution(817815399761112421)
XLA Ops:
  0.6 72.3 %shard_map.93 = (bf16[2,6,128,512]{3,2,1,0:T(8,128)(2,1)S(1)}, bf16[6,128,2048]{2,1,0:T(8,128)(2,1)S(1)}) custom-call(s32[28]{0:T(128)} %old_ref.1, s32[28]{0:T(128)} %new_ref.1, bf16[1,4,128,2048]{3,2,1,0:T(8,128)(2,1)} %g_hbm.1, f32[4,128,512]{2,1,0:T(8,128)} %m_hbm.1, f32[4,128,512]{2,1,0:T(8,128)} %v_hbm.1, f32[4,128,512]{2,1,0:T(8,128)} %w_hbm.1), custom_call_target="tpu_custom_call" | custom-call | tf_op jit(solution)/shard_map/pallas_call | solution.py:415
  72.9 3.3 %shard_map.94 = (f32[6,128,512]{2,1,0:T(8,128)}, f32[6,128,512]{2,1,0:T(8,128)}, f32[6,128,512]{2,1,0:T(8,128)}, bf16[6,128,2048]{2,1,0:T(8,128)(2,1)}) custom-call(bf16[2,6,128,512]{3,2,1,0:T(8,128)(2,1)S(1)} %get-tuple-element.6.moments, bf16[6,128,2048]{2,1,0:T(8,128)(2,1)S(1)} %get-tuple-element.7.params), custom_call_target="tpu_custom_call" | custom-call | tf_op jit(solution)/shard_map/pallas_call | solution.py:428

commit v4 on v3

--- a/solution.py
+++ b/solution.py
@@ -10,32 +10,43 @@
 
 MESH = pl.DeviceIdType.MESH
 ROWS = 16
-KINDS = 'UDXMWFVZ'
-PARTS = (1, 1, 1, 1, 1, 1, 1, 1)
-EARLY = (0, 1, 1, 1, 0, 1, 0, 0)
-SPLIT = (1, 0, 0, 0, 0, 0, 0, 1)
+KINDS = 'UDXMWFVZA'
+PARTS = (2, 2, 2, 2, 2, 2, 2, 2)
+EARLY = (0, 0, 0, 1, 1, 0, 1, 0, 1, 1, 0, 1, 0, 1, 1, 0)
+SPLIT = (1, 1, 0, 0, 0, 0, 0, 0, 0, 0, 0, 0, 0, 0, 0, 0)
+AHEAD = (0, 0, 0, 0, 0, 0, 0, 0, 0, 0, 0, 0, 0, 0, 0, 0)
 ORDERS = (
     (
-        13, 43, 2, 3, 23, 1, 12, 33, 42, 11, 2010, 41, 63, 62, 53, 3010, 73, 2040, 61, 3040, 2000, 22, 52, 2020,
-        21, 3020, 51, 32, 4000, 72, 2030, 3000, 3030, 4010, 2060, 3060, 2050, 71, 3050, 2070, 4070, 31, 6000,
-        6040, 6060, 4020, 6010, 6070, 4050, 4030, 6020, 3070, 6050, 6030, 7040, 7000, 7070, 7060,
+        32, 2, 33, 23, 123, 1, 92, 13, 73, 31, 12, 91, 93, 3, 11, 43, 22, 2030, 52, 153, 113, 21, 53, 3030,
+        2020, 63, 3020, 2120, 3120, 2010, 4010, 3010, 51, 42, 122, 2070, 83, 3070, 121, 72, 2000, 41, 103, 143,
+        3000, 2090, 71, 62, 4030, 133, 2040, 152, 3040, 3090, 2050, 61, 2150, 151, 2060, 2110, 3050, 82, 112,
+        141, 142, 4000, 3150, 111, 4090, 132, 2140, 81, 102, 6150, 101, 6010, 3110, 4040, 131, 6050, 2100, 6030,
+        6000, 6120, 2130, 6070, 2080, 3130, 3080, 6040, 3100, 3060, 3140, 4060, 6020, 6100, 4110, 4140, 6110,
+        4080, 4130, 6090, 6140, 6080, 7050, 7070, 7000, 7010, 6060, 7150, 7100, 7120, 6130, 7020,
     ),
     (
-        13, 43, 2, 1010, 3, 23, 1040, 2000, 4000, 12, 1000, 33, 1020, 3000, 42, 6000, 2010, 3010, 1030, 5010,
-        2040, 3040, 63, 5002, 62, 5012, 53, 5013, 4010, 73, 7000, 1060, 6040, 2060, 22, 1050, 52, 1070, 3060,
-        5020, 5042, 2020, 3020, 2050, 3050, 32, 72, 5023, 5022, 4020, 5052, 5050, 6060, 2070, 5030, 2030, 4070,
-        3070, 3030, 5053, 5000, 5062, 5033, 5040, 5032, 4030, 6070, 6010, 5070, 7070, 5043, 6020, 5060, 5072,
-        4050, 5073, 5003, 5063, 6030, 6050,
+        32, 2, 33, 23, 123, 2000, 4000, 1030, 92, 1020, 13, 1120, 73, 3000, 2030, 3030, 12, 6000, 93, 1010, 3,
+        1070, 2090, 5032, 2010, 4010, 43, 22, 5002, 3010, 3090, 5030, 1090, 52, 1000, 153, 5092, 1040, 113,
+        2020, 3020, 53, 5033, 6010, 63, 2050, 3050, 1150, 42, 1110, 122, 1050, 4030, 83, 6020, 1060, 72, 5012,
+        2040, 2120, 3120, 143, 1080, 5090, 6050, 3040, 2070, 103, 5042, 62, 5022, 7000, 3070, 5093, 5040, 133,
+        4090, 1140, 6120, 5060, 1100, 152, 5110, 5043, 2060, 6070, 1130, 5052, 4040, 112, 82, 2150, 5063, 142,
+        3150, 5113, 5140, 3060, 5062, 2110, 2080, 5072, 4060, 132, 102, 5150, 2140, 3110, 6150, 3080, 5143,
+        5122, 5112, 6030, 3140, 2130, 2100, 5050, 5130, 5142, 3100, 5000, 3130, 5082, 5010, 5153, 5080, 5132,
+        5053, 4140, 5120, 5133, 6040, 5152, 5070, 5100, 5083, 5003, 6060, 4080, 4130, 6100, 4110, 5123, 5103,
+        5073, 5020, 5013, 7010, 6080, 6140, 5102, 5023, 6090, 6130, 6110,
     ),
 )
 
 
-def adam_step(gradient, moment_one, moment_two, weight):
+def moment_step(gradient, moment_one, moment_two):
     moment_one = 0.9 * moment_one + 0.1 * gradient
     moment_two = 0.95 * moment_two + 0.05 * gradient * gradient
+    return moment_one, moment_two
+
+
+def weight_step(moment_one, moment_two, weight):
     update = moment_one / (1.0 - 0.9**50) / (jnp.sqrt(moment_two / (1.0 - 0.95**50)) + 1e-08)
-    weight = weight - 0.05 * (update + 0.1 * weight)
-    return (weight, moment_one, moment_two)
+    return weight - 0.05 * (update + 0.1 * weight)
 
 
 class Chunk(typing.NamedTuple):
@@ -44,6 +55,7 @@
     width: int
     early: bool
     split: bool
+    ahead: bool
 
 
 def job_list(dp, chunks, role):
@@ -56,7 +68,7 @@
         if chunk.early:
             jobs += [("M", c, 0)] + passed + [("W", c, 0), ("V", c, 0)]
         else:
-            jobs += [("W", c, 0)] * chunk.split + [("M", c, 0), ("V", c, 0)] + passed
+            jobs += [("A", c, 0)] * chunk.ahead + [("W", c, 0)] * chunk.split + [("M", c, 0), ("V", c, 0)] + passed
             jobs += [("Z", c, 0)] * (chunk.split or role == 0)
     return jobs
 
@@ -66,7 +78,7 @@
     parts = PARTS if tuned else (1,) * (tile_rows // ROWS)
     spans = [(i * ROWS, j * (cols // n), cols // n) for i, n in enumerate(parts) for j in range(n)]
     chunks = [
-        Chunk(*span, *((EARLY[c] == 1, SPLIT[c] == 1) if tuned else (c % 2 == 0, False)))
+        Chunk(*span, *((EARLY[c] == 1, SPLIT[c] == 1, AHEAD[c] == 1) if tuned else (c % 2 == 0, False, False)))
         for c, span in enumerate(spans)
     ]
     orders = [job_list(dp, chunks, role) for role in range(dp // 2)]
@@ -83,7 +95,7 @@
     rest = rest[4:]
     count = len(chunks)
     fresh, mail, inbox, wide, wide_mail, wide_inbox = (rest[i * count : (i + 1) * count] for i in range(6))
-    (g_sem, in_sem, s_send, s_recv, a_send, a_recv, x_send, x_recv, w_send, w_recv) = rest[6 * count :]
+    (g_sem, in_sem, sent, z_recv, x_recv, w_recv) = rest[6 * count :]
     z = lax.axis_index("dp")
     e = lax.axis_index("expert")
     old_slots, cols = state.shape[1], state.shape[-1]
@@ -124,6 +136,16 @@
     def beside(right):
         return {"dp": z + ahead if right else z - ahead}
 
+    g_loads = [
+        pltpu.make_async_copy(g_hbm.at[0, :, pl.ds(row, ROWS)], g.at[:, pl.ds(row, ROWS)], g_sem.at[row // ROWS])
+        for row in range(0, g.shape[1], ROWS)
+    ]
+    loads = [pltpu.make_async_copy(ref, state.at[i], in_sem) for i, ref in enumerate((m_hbm, v_hbm, w_hbm))]
+
+    @pl.when(owns)
+    def _():
+        g_loads[0].start()
+
     barrier = pltpu.get_barrier_semaphore()
     for to in targets[1:]:
         pl.semaphore_signal(barrier, inc=1, device_id={"expert": to}, device_id_type=MESH)
@@ -132,17 +154,9 @@
         def _():
             pl.semaphore_signal(barrier, inc=1, device_id={"dp": z + step}, device_id_type=MESH)
 
-    g_loads = [
-        pltpu.make_async_copy(g_hbm.at[0, :, pl.ds(row, ROWS)], g.at[:, pl.ds(row, ROWS)], g_sem.at[row // ROWS])
-        for row in range(0, g.shape[1], ROWS)
-    ]
-    loads = [
-        pltpu.make_async_copy(ref, state.at[i], in_sem) for i, ref in enumerate((m_hbm, v_hbm, w_hbm))
-    ]
-
     @pl.when(owns)
     def _():
-        for load in g_loads[:1] + loads + g_loads[1:]:
+        for load in loads + g_loads[1:]:
             load.start()
 
     inner = (z > 0).astype(jnp.int32) + (z < dp - 1).astype(jnp.int32)
@@ -164,14 +178,14 @@
     def sum_copy(c, k, right, raw=False):
         src = g.at[:, rows(c), block(c, k)] if raw else part.at[real(k), :, rows(c), span(c)]
         return pltpu.make_async_remote_copy(
-            src, line.at[way(right), real(k), :, rows(c), span(c)], s_send, s_recv.at[c, real(k)],
+            src, line.at[way(right), real(k), :, rows(c), span(c)], sent, z_recv.at[c, real(k)],
             device_id=beside(right), device_id_type=MESH,
         )
 
     def gather_copy(c, k, right, to_end):
         where = wide[c].at[:, :, wide_block(c, real(k))] if chunks[c].early else params.at[:, rows(c), block(c, k)]
         return pltpu.make_async_remote_copy(
-            where, where, a_send.at[c], a_recv.at[c, real(0 if to_end else k)],
+            where, where, sent, z_recv.at[c, real(1 if to_end else k)],
             device_id=beside(right), device_id_type=MESH,
         )
 
@@ -184,7 +198,7 @@
 
     def mail_copy(c, to):
         return pltpu.make_async_remote_copy(
-            mail[c].at[to], inbox[c].at[e], x_send.at[c], x_recv.at[c],
+            mail[c].at[to], inbox[c].at[e], sent, x_recv.at[c],
             device_id={"expert": to}, device_id_type=MESH,
         )
 
@@ -193,7 +207,7 @@
 
     def weights_copy(c, to):
         return pltpu.make_async_remote_copy(
-            wide_mail[c].at[to], wide_inbox[c].at[e], w_send.at[c], w_recv.at[c],
+            wide_mail[c].at[to], wide_inbox[c].at[e], sent, w_recv.at[c],
             device_id={"expert": to}, device_id_type=MESH,
         )
 
@@ -217,12 +231,14 @@
     def update(c, role):
         sides = [right for right in (True, False) if role > 0 or not right]
         at = line.at[pl.ds(0, len(sides)), z, :, rows(c), span(c)]
-        taken_by(s_recv.at[c, z], at)
+        taken_by(z_recv.at[c, z], at)
         for slot in range(old_slots):
             gradient = g[slot, rows(c), mine(c)].astype(jnp.float32)
             for right in sides:
                 gradient += line[way(right), z, slot, rows(c), span(c)].astype(jnp.float32)
-            values = adam_step(gradient, *(state[i, slot, rows(c), span(c)] for i in range(3)))
+            values = list(moment_step(gradient, *(state[i, slot, rows(c), span(c)] for i in range(2))))
+            if not chunks[c].ahead:
+                values.insert(0, weight_step(*values, state[2, slot, rows(c), span(c)]))
             values = [value.astype(jnp.bfloat16) for value in values]
             if chunks[c].early:
                 wide[c][slot, :, wide_block(c, z)] = values.pop(0)
@@ -241,7 +257,13 @@
 
     def last_arrivals(c, role):
         if role == 0:
-            taken_by(a_recv.at[c, z], gather_bytes(c, dp - 1))
+            taken_by(z_recv.at[c, real(1)], gather_bytes(c, dp - 1))
+
+    def post_old_weights(c, slots):
+        for to, slot in zip(targets[1:], slots[1:]):
+            wide_mail[c][to] = state[2, slot, rows(c), span(c)].astype(jnp.bfloat16)
+            weights_copy(c, to).start()
+        wide_inbox[c][e] = state[2, slots[0], rows(c), span(c)].astype(jnp.bfloat16)
 
     def post_weights(c, role, slots):
         if chunks[c].early:
@@ -270,14 +292,20 @@
                 moments[i, slot, rows(c), span(c)] = kept(slot, taken, inbox[c][sources[slot], first + i])
 
     def deliver(c, role, taken, sources):
-        receive(c, not chunks[c].split, chunks[c].early or chunks[c].split)
+        receive(c, not chunks[c].split, chunks[c].early or chunks[c].split or chunks[c].ahead)
         for slot in range(new_slots):
             if chunks[c].early:
                 for k in range(dp):
                     value = wide_inbox[c][sources[slot], :, wide_block(c, k)]
                     params[slot, rows(c), pl.ds(k * cols + chunks[c].col, chunks[c].width)] = kept(slot, taken, value)
             else:
-                box = wide_inbox[c][sources[slot]] if chunks[c].split else inbox[c][sources[slot], 0]
+                if chunks[c].ahead:
+                    values = [inbox[c][sources[slot], i] for i in range(2)] + [wide_inbox[c][sources[slot]]]
+                    box = weight_step(*(value.astype(jnp.float32) for value in values)).astype(jnp.bfloat16)
+                elif chunks[c].split:
+                    box = wide_inbox[c][sources[slot]]
+                else:
+                    box = inbox[c][sources[slot], 0]
                 params[slot, rows(c), mine(c)] = kept(slot, taken, box)
         if not chunks[c].early:
             gather(c, role)
@@ -292,13 +320,13 @@
 
     def run(role, order, slots, taken, sources, loaded):
         for kind, c, k in order:
-            by_owners = kind in "UDXMW" or (kind == "F" and chunks[c].early)
+            by_owners = kind in "UDXMWA" or (kind == "F" and chunks[c].early)
 
             def job():
                 if kind in "UDX" and chunks[c].row not in loaded:
                     loaded.append(chunks[c].row)
                     g_loads[chunks[c].row // ROWS].wait()
-                if kind == "X" and -1 not in loaded:
+                if kind in "XA" and -1 not in loaded:
                     loaded.append(-1)
                     taken_by(in_sem, state)
                 if kind == "U" and role == 0:
@@ -307,6 +335,8 @@
                     add_and_send(c, k, kind == "U")
                 elif kind == "X":
                     update(c, role)
+                elif kind == "A":
+                    post_old_weights(c, slots)
                 elif kind == "M":
                     post(c, slots)
                 elif kind == "F":
@@ -346,7 +376,7 @@
             run(role, order[lead:] if role == 0 else order, slots, taken, sources, loaded[role])
 
             def gathers_sent(c):
-                taken_by(a_send.at[c], gather_bytes(c, dp + 1 if role > 0 else 1))
+                taken_by(sent, gather_bytes(c, dp + 1 if role > 0 else 1))
 
             for c in range(count):
                 if not chunks[c].early:
@@ -360,27 +390,25 @@
 
     @pl.when(owns)
     def _():
-        taken_by(s_send, part.at[pl.ds(0, dp - 1)])
+        taken_by(sent, part.at[pl.ds(0, dp - 1)])
         for c in range(count):
-            taken_by(x_send.at[c], mail_bytes(c, peers - 1))
-            if chunks[c].early or chunks[c].split:
-                taken_by(w_send.at[c], weights_bytes(c, peers - 1))
-
-
-def widen(moments, params, w_out, m_out, v_out, p_out, staged, sems, sem):
+            taken_by(sent, mail_bytes(c, peers - 1))
+            if chunks[c].early or chunks[c].split or chunks[c].ahead:
+                taken_by(sent, weights_bytes(c, peers - 1))
+
+
+def widen(moments, params, w_out, m_out, v_out, p_out, staged, sems):
     new_slots, _, cols = w_out.shape
     z = lax.axis_index("dp")
     mine = pl.ds(pl.multiple_of(z * cols, cols), cols)
-    copies = [pltpu.make_async_copy(params, p_out, sem)]
-    copies[0].start()
+    pltpu.make_async_copy(params, p_out, sems.at[3]).start()
     for slot in range(new_slots):
         parts = (params.at[slot, :, mine], moments.at[0, slot], moments.at[1, slot])
         for i, (part, out) in enumerate(zip(parts, (w_out, m_out, v_out))):
             staged[i, slot] = part[...].astype(jnp.float32)
-            copies.append(pltpu.make_async_copy(staged.at[i, slot], out.at[slot], sems.at[i, slot]))
-            copies[-1].start()
-    for copy in copies:
-        copy.wait()
+            pltpu.make_async_copy(staged.at[i, slot], out.at[slot], sems.at[i]).start()
+    for i, out in enumerate((w_out, m_out, v_out, p_out)):
+        pltpu.make_async_copy(out, out, sems.at[i]).wait()
 
 
 def shards(grad_parts, first_moment, second_moment, master_weight, old_owner, new_owner):
@@ -403,14 +431,15 @@
         pltpu.VMEM((dp, old_slots, tile_rows, cols), bf16),
         pltpu.VMEM((2, dp, old_slots, tile_rows, cols), bf16),
     ]
-    kept = [2 if chunk.early or chunk.split else 3 for chunk in chunks]
-    wide = [chunk.width * (dp if chunk.early else 1) if chunk.early or chunk.split else 128 for chunk in chunks]
+    apart = [chunk.early or chunk.split or chunk.ahead for chunk in chunks]
+    kept = [2 if flag else 3 for flag in apart]
+    wide = [chunk.width * (dp if chunk.early else 1) if flag else 128 for flag, chunk in zip(apart, chunks)]
     for boxes in (old_slots, peers, owners):
         scratch += [pltpu.VMEM((boxes, n, ROWS, chunk.width), bf16) for n, chunk in zip(kept, chunks)]
     for boxes in (old_slots, peers, owners):
         scratch += [pltpu.VMEM((boxes, ROWS, n), bf16) for n in wide]
-    scratch += [dma((tile_rows // ROWS,)), dma, dma] + [dma((count, dp)), dma((count,)), dma((count, dp))]
-    scratch += [dma((count,))] * 4
+    scratch += [dma((tile_rows // ROWS,)), dma, dma, dma((count, dp))]
+    scratch += [dma((count,))] * 2
     results = new_slots * tile_rows * cols * (4 + 2 * dp)
     moments, params = pl.pallas_call(
         functools.partial(kernel, dp, peers, owners, chunks, orders),
@@ -431,7 +460,7 @@
         + (jax.ShapeDtypeStruct((new_slots, tile_rows, dp * cols), bf16),),
         in_specs=[vmem] * 2,
         out_specs=(any_space,) * 4,
-        scratch_shapes=[pltpu.VMEM((3, new_slots, tile_rows, cols), f32), dma((3, new_slots)), dma],
+        scratch_shapes=[pltpu.VMEM((3, new_slots, tile_rows, cols), f32), dma((4,))],
         compiler_params=pltpu.CompilerParams(vmem_limit_bytes=2**24),
     )(moments, params)
 

time: 76.4 us -> 74.2 us (0.971)
  Pallas kernels: 75.6 us -> 73.4 us
    pallas_call x1, Pallas kernels: 72.3 us -> 70.3 us  [shards(): pl.pallas_call(functools.partial(kernel, dp, peers, owners, chunks, order...]
where the time goes in v4:
time: 74.2 us; the launch traced here: 74.1 us
  Pallas kernels  73.4 us (99%)
    pallas_call x1, Pallas kernels, shards(): pl.pallas_call(functools.partial(kernel, dp, peers, owners, chunks, order...  70.3 us
    pallas_call x1, Pallas kernels, shards(): pl.pallas_call(widen, out_shape=(master,) * 3 + (jax.ShapeDtypeStruct((ne...  3.14 us

profile of v4, /device:TPU:0, one launch (start us, length us, event | category | flops | bytes accessed | tf_op | source)
XLA Modules:
  0.0 74.1 jit_solution(18065745426784422232)
XLA Ops:
  0.6 70.3 %shard_map.93 = (bf16[2,6,128,512]{3,2,1,0:T(8,128)(2,1)S(1)}, bf16[6,128,2048]{2,1,0:T(8,128)(2,1)S(1)}) custom-call(s32[28]{0:T(128)} %old_ref.1, s32[28]{0:T(128)} %new_ref.1, bf16[1,4,128,2048]{3,2,1,0:T(8,128)(2,1)} %g_hbm.1, f32[4,128,512]{2,1,0:T(8,128)} %m_hbm.1, f32[4,128,512]{2,1,0:T(8,128)} %v_hbm.1, f32[4,128,512]{2,1,0:T(8,128)} %w_hbm.1), custom_call_target="tpu_custom_call" | custom-call | tf_op jit(solution)/shard_map/pallas_call | solution.py:444
  70.9 3.1 %shard_map.94 = (f32[6,128,512]{2,1,0:T(8,128)}, f32[6,128,512]{2,1,0:T(8,128)}, f32[6,128,512]{2,1,0:T(8,128)}, bf16[6,128,2048]{2,1,0:T(8,128)(2,1)}) custom-call(bf16[2,6,128,512]{3,2,1,0:T(8,128)(2,1)S(1)} %get-tuple-element.6.moments, bf16[6,128,2048]{2,1,0:T(8,128)(2,1)S(1)} %get-tuple-element.7.params), custom_call_target="tpu_custom_call" | custom-call | tf_op jit(solution)/shard_map/pallas_call | solution.py:457

commit v5 on v4

--- a/solution.py
+++ b/solution.py
@@ -11,29 +11,24 @@
 MESH = pl.DeviceIdType.MESH
 ROWS = 16
 KINDS = 'UDXMWFVZA'
-PARTS = (2, 2, 2, 2, 2, 2, 2, 2)
-EARLY = (0, 0, 0, 1, 1, 0, 1, 0, 1, 1, 0, 1, 0, 1, 1, 0)
-SPLIT = (1, 1, 0, 0, 0, 0, 0, 0, 0, 0, 0, 0, 0, 0, 0, 0)
-AHEAD = (0, 0, 0, 0, 0, 0, 0, 0, 0, 0, 0, 0, 0, 0, 0, 0)
+PARTS = (2, 2, 2, 1, 1, 1, 1, 1)
+EARLY = (0, 0, 1, 0, 1, 1, 1, 1, 0, 1, 0)
+SPLIT = (0, 0, 0, 0, 0, 0, 0, 0, 0, 0, 0)
+AHEAD = (0, 1, 0, 0, 0, 0, 0, 0, 1, 0, 1)
 ORDERS = (
     (
-        32, 2, 33, 23, 123, 1, 92, 13, 73, 31, 12, 91, 93, 3, 11, 43, 22, 2030, 52, 153, 113, 21, 53, 3030,
-        2020, 63, 3020, 2120, 3120, 2010, 4010, 3010, 51, 42, 122, 2070, 83, 3070, 121, 72, 2000, 41, 103, 143,
-        3000, 2090, 71, 62, 4030, 133, 2040, 152, 3040, 3090, 2050, 61, 2150, 151, 2060, 2110, 3050, 82, 112,
-        141, 142, 4000, 3150, 111, 4090, 132, 2140, 81, 102, 6150, 101, 6010, 3110, 4040, 131, 6050, 2100, 6030,
-        6000, 6120, 2130, 6070, 2080, 3130, 3080, 6040, 3100, 3060, 3140, 4060, 6020, 6100, 4110, 4140, 6110,
-        4080, 4130, 6090, 6140, 6080, 7050, 7070, 7000, 7010, 6060, 7150, 7100, 7120, 6130, 7020,
+        12, 23, 8080, 43, 22, 8010, 3, 11, 8100, 33, 13, 2, 21, 42, 53, 63, 1, 41, 2020, 2040, 3020, 3040, 32,
+        2000, 62, 2030, 73, 3030, 31, 3000, 61, 2050, 52, 3050, 83, 82, 2010, 51, 3010, 2060, 81, 103, 3060, 93,
+        4020, 4040, 72, 92, 2070, 3070, 71, 91, 6030, 6020, 6000, 2080, 102, 3080, 4050, 6010, 2100, 3100, 2090,
+        4060, 101, 6040, 6050, 3090, 6080, 6100, 4070, 4090, 7000, 6070, 7010, 7030, 6060, 6090, 7080, 7100,
     ),
     (
-        32, 2, 33, 23, 123, 2000, 4000, 1030, 92, 1020, 13, 1120, 73, 3000, 2030, 3030, 12, 6000, 93, 1010, 3,
-        1070, 2090, 5032, 2010, 4010, 43, 22, 5002, 3010, 3090, 5030, 1090, 52, 1000, 153, 5092, 1040, 113,
-        2020, 3020, 53, 5033, 6010, 63, 2050, 3050, 1150, 42, 1110, 122, 1050, 4030, 83, 6020, 1060, 72, 5012,
-        2040, 2120, 3120, 143, 1080, 5090, 6050, 3040, 2070, 103, 5042, 62, 5022, 7000, 3070, 5093, 5040, 133,
-        4090, 1140, 6120, 5060, 1100, 152, 5110, 5043, 2060, 6070, 1130, 5052, 4040, 112, 82, 2150, 5063, 142,
-        3150, 5113, 5140, 3060, 5062, 2110, 2080, 5072, 4060, 132, 102, 5150, 2140, 3110, 6150, 3080, 5143,
-        5122, 5112, 6030, 3140, 2130, 2100, 5050, 5130, 5142, 3100, 5000, 3130, 5082, 5010, 5153, 5080, 5132,
-        5053, 4140, 5120, 5133, 6040, 5152, 5070, 5100, 5083, 5003, 6060, 4080, 4130, 6100, 4110, 5123, 5103,
-        5073, 5020, 5013, 7010, 6080, 6140, 5102, 5023, 6090, 6130, 6110,
+        12, 8010, 23, 43, 3, 22, 8100, 2010, 3010, 33, 1020, 1040, 13, 1000, 2, 2020, 42, 1030, 53, 3020, 1010,
+        6010, 5022, 63, 8080, 2000, 3000, 2040, 5040, 1050, 5012, 3040, 32, 5020, 1060, 62, 5042, 5043, 4040,
+        6000, 73, 2030, 3030, 5023, 2060, 52, 5050, 5002, 3060, 83, 1070, 4020, 82, 6030, 2050, 3050, 5053,
+        5060, 1080, 5062, 2080, 103, 3080, 5032, 93, 6020, 5052, 5063, 4060, 72, 1100, 4050, 92, 1090, 5070,
+        6080, 2090, 6040, 3090, 5073, 2070, 6060, 102, 3070, 5030, 5082, 5090, 5072, 2100, 5092, 3100, 5000,
+        5033, 5010, 4070, 5080, 5093, 5003, 4090, 5013, 5100, 6100, 5083, 6050, 5103, 5102, 6070, 6090,
     ),
 )
 
@@ -66,7 +61,7 @@
         if role > 0:
             passed += [("F", c, k) for k in range(role + 1, dp)]
         if chunk.early:
-            jobs += [("M", c, 0)] + passed + [("W", c, 0), ("V", c, 0)]
+            jobs += [("A", c, 0)] * chunk.ahead + [("M", c, 0)] + passed + [("W", c, 0), ("V", c, 0)]
         else:
             jobs += [("A", c, 0)] * chunk.ahead + [("W", c, 0)] * chunk.split + [("M", c, 0), ("V", c, 0)] + passed
             jobs += [("Z", c, 0)] * (chunk.split or role == 0)
@@ -94,8 +89,10 @@
     g, state, part, line = rest[:4]
     rest = rest[4:]
     count = len(chunks)
-    fresh, mail, inbox, wide, wide_mail, wide_inbox = (rest[i * count : (i + 1) * count] for i in range(6))
-    (g_sem, in_sem, sent, z_recv, x_recv, w_recv) = rest[6 * count :]
+    fresh, mail, inbox, wide, wide_mail, wide_inbox, old_mail, old_inbox = (
+        rest[i * count : (i + 1) * count] for i in range(8)
+    )
+    g_sem, in_sem, sent, z_recv, x_recv, w_recv, o_recv = rest[8 * count :]
     z = lax.axis_index("dp")
     e = lax.axis_index("expert")
     old_slots, cols = state.shape[1], state.shape[-1]
@@ -124,8 +121,8 @@
     def block(c, k):
         return pl.ds(pl.multiple_of(real(k) * cols + chunks[c].col, 128), chunks[c].width)
 
-    def wide_block(c, k):
-        return pl.ds(pl.multiple_of(k * chunks[c].width, 128), chunks[c].width)
+    def wide_block(c, k, plane):
+        return pl.ds(pl.multiple_of(lax.rem(k - plane + dp, dp) * chunks[c].width, 128), chunks[c].width)
 
     def mine(c):
         return pl.ds(pl.multiple_of(z * cols + chunks[c].col, 128), chunks[c].width)
@@ -183,9 +180,12 @@
         )
 
     def gather_copy(c, k, right, to_end):
-        where = wide[c].at[:, :, wide_block(c, real(k))] if chunks[c].early else params.at[:, rows(c), block(c, k)]
+        src = dst = params.at[:, rows(c), block(c, k)]
+        if chunks[c].early:
+            src = wide[c].at[:, :, wide_block(c, real(k), z)]
+            dst = wide[c].at[:, :, wide_block(c, real(k), beside(right)["dp"])]
         return pltpu.make_async_remote_copy(
-            where, where, sent, z_recv.at[c, real(1 if to_end else k)],
+            src, dst, sent, z_recv.at[c, real(1 if to_end else k)],
             device_id=beside(right), device_id_type=MESH,
         )
 
@@ -208,6 +208,12 @@
     def weights_copy(c, to):
         return pltpu.make_async_remote_copy(
             wide_mail[c].at[to], wide_inbox[c].at[e], sent, w_recv.at[c],
+            device_id={"expert": to}, device_id_type=MESH,
+        )
+
+    def old_copy(c, to):
+        return pltpu.make_async_remote_copy(
+            old_mail[c].at[to], old_inbox[c].at[e], sent, o_recv.at[c],
             device_id={"expert": to}, device_id_type=MESH,
         )
 
@@ -237,11 +243,11 @@
             for right in sides:
                 gradient += line[way(right), z, slot, rows(c), span(c)].astype(jnp.float32)
             values = list(moment_step(gradient, *(state[i, slot, rows(c), span(c)] for i in range(2))))
-            if not chunks[c].ahead:
+            if chunks[c].early or not chunks[c].ahead:
                 values.insert(0, weight_step(*values, state[2, slot, rows(c), span(c)]))
             values = [value.astype(jnp.bfloat16) for value in values]
             if chunks[c].early:
-                wide[c][slot, :, wide_block(c, z)] = values.pop(0)
+                wide[c][slot, :, pl.ds(0, chunks[c].width)] = values.pop(0)
             elif chunks[c].split:
                 wide[c][slot] = values.pop(0)
             for i, value in enumerate(values):
@@ -261,19 +267,21 @@
 
     def post_old_weights(c, slots):
         for to, slot in zip(targets[1:], slots[1:]):
-            wide_mail[c][to] = state[2, slot, rows(c), span(c)].astype(jnp.bfloat16)
-            weights_copy(c, to).start()
-        wide_inbox[c][e] = state[2, slots[0], rows(c), span(c)].astype(jnp.bfloat16)
+            old_mail[c][to] = state[2, slot, rows(c), span(c)].astype(jnp.bfloat16)
+            old_copy(c, to).start()
+        old_inbox[c][e] = state[2, slots[0], rows(c), span(c)].astype(jnp.bfloat16)
 
     def post_weights(c, role, slots):
         if chunks[c].early:
             last_arrivals(c, role)
+        size = wide_mail[c].shape[2]
+        columns = pl.ds(wide[c].shape[2] - size, size)
         for to, slot in zip(targets[1:], slots[1:]):
-            wide_mail[c][to] = wide[c][slot]
+            wide_mail[c][to] = wide[c][slot, :, columns]
             weights_copy(c, to).start()
-        wide_inbox[c][e] = wide[c][slots[0]]
-
-    def receive(c, moments_too, weights_too):
+        wide_inbox[c][e] = wide[c][slots[0], :, columns]
+
+    def receive(c, moments_too, weights_too, old_too):
         for mask, boxes in ((owns, owners - 1), (e >= owners, owners)):
             @pl.when(mask)
             def _():
@@ -281,6 +289,8 @@
                     taken_by(x_recv.at[c], mail_bytes(c, boxes))
                 if weights_too:
                     taken_by(w_recv.at[c], weights_bytes(c, boxes))
+                if old_too:
+                    taken_by(o_recv.at[c], old_mail[c].at[pl.ds(0, boxes)])
 
     def kept(slot, taken, value):
         return jnp.where(taken > slot, value, jnp.zeros_like(value))
@@ -292,21 +302,22 @@
                 moments[i, slot, rows(c), span(c)] = kept(slot, taken, inbox[c][sources[slot], first + i])
 
     def deliver(c, role, taken, sources):
-        receive(c, not chunks[c].split, chunks[c].early or chunks[c].split or chunks[c].ahead)
+        width = chunks[c].width
+        receive(c, not chunks[c].split, chunks[c].early or chunks[c].split, chunks[c].ahead)
         for slot in range(new_slots):
-            if chunks[c].early:
-                for k in range(dp):
-                    value = wide_inbox[c][sources[slot], :, wide_block(c, k)]
-                    params[slot, rows(c), pl.ds(k * cols + chunks[c].col, chunks[c].width)] = kept(slot, taken, value)
+            if chunks[c].ahead:
+                values = [inbox[c][sources[slot], i] for i in range(2)] + [old_inbox[c][sources[slot]]]
+                own = weight_step(*(value.astype(jnp.float32) for value in values)).astype(jnp.bfloat16)
+            elif chunks[c].early:
+                own = wide_inbox[c][sources[slot], :, pl.ds(0, width)]
             else:
-                if chunks[c].ahead:
-                    values = [inbox[c][sources[slot], i] for i in range(2)] + [wide_inbox[c][sources[slot]]]
-                    box = weight_step(*(value.astype(jnp.float32) for value in values)).astype(jnp.bfloat16)
-                elif chunks[c].split:
-                    box = wide_inbox[c][sources[slot]]
-                else:
-                    box = inbox[c][sources[slot], 0]
-                params[slot, rows(c), mine(c)] = kept(slot, taken, box)
+                own = wide_inbox[c][sources[slot]] if chunks[c].split else inbox[c][sources[slot], 0]
+            params[slot, rows(c), mine(c)] = kept(slot, taken, own)
+            for step in range(1, dp if chunks[c].early else 1):
+                column = pl.multiple_of(lax.rem(z + step, dp) * cols + chunks[c].col, 128)
+                first = (step - 1 if chunks[c].ahead else step) * width
+                value = wide_inbox[c][sources[slot], :, pl.ds(first, width)]
+                params[slot, rows(c), pl.ds(column, width)] = kept(slot, taken, value)
         if not chunks[c].early:
             gather(c, role)
         if not chunks[c].split:
@@ -314,7 +325,7 @@
 
     def finish(c, role, taken, sources):
         if chunks[c].split:
-            receive(c, True, False)
+            receive(c, True, False, False)
             place_moments(c, taken, sources)
         last_arrivals(c, role)
 
@@ -393,8 +404,10 @@
         taken_by(sent, part.at[pl.ds(0, dp - 1)])
         for c in range(count):
             taken_by(sent, mail_bytes(c, peers - 1))
-            if chunks[c].early or chunks[c].split or chunks[c].ahead:
+            if chunks[c].early or chunks[c].split:
                 taken_by(sent, weights_bytes(c, peers - 1))
+            if chunks[c].ahead:
+                taken_by(sent, old_mail[c].at[pl.ds(0, peers - 1)])
 
 
 def widen(moments, params, w_out, m_out, v_out, p_out, staged, sems):
@@ -431,15 +444,16 @@
         pltpu.VMEM((dp, old_slots, tile_rows, cols), bf16),
         pltpu.VMEM((2, dp, old_slots, tile_rows, cols), bf16),
     ]
-    apart = [chunk.early or chunk.split or chunk.ahead for chunk in chunks]
-    kept = [2 if flag else 3 for flag in apart]
-    wide = [chunk.width * (dp if chunk.early else 1) if flag else 128 for flag, chunk in zip(apart, chunks)]
+    kept = [2 if chunk.early or chunk.split or chunk.ahead else 3 for chunk in chunks]
+    wide = [chunk.width * (dp if chunk.early else 1) if chunk.early or chunk.split else 128 for chunk in chunks]
+    sent = [size - chunk.width if chunk.early and chunk.ahead else size for size, chunk in zip(wide, chunks)]
+    old = [chunk.width if chunk.ahead else 128 for chunk in chunks]
     for boxes in (old_slots, peers, owners):
         scratch += [pltpu.VMEM((boxes, n, ROWS, chunk.width), bf16) for n, chunk in zip(kept, chunks)]
-    for boxes in (old_slots, peers, owners):
-        scratch += [pltpu.VMEM((boxes, ROWS, n), bf16) for n in wide]
+    for boxes, sizes in ((old_slots, wide), (peers, sent), (owners, sent), (peers, old), (owners, old)):
+        scratch += [pltpu.VMEM((boxes, ROWS, n), bf16) for n in sizes]
     scratch += [dma((tile_rows // ROWS,)), dma, dma, dma((count, dp))]
-    scratch += [dma((count,))] * 2
+    scratch += [dma((count,))] * 3
     results = new_slots * tile_rows * cols * (4 + 2 * dp)
     moments, params = pl.pallas_call(
         functools.partial(kernel, dp, peers, owners, chunks, orders),

time: 74.2 us -> 73.1 us (0.985)
  Pallas kernels: 73.4 us -> 72.3 us
    pallas_call x1, Pallas kernels: 70.3 us -> 69.1 us  [shards(): pl.pallas_call(functools.partial(kernel, dp, peers, owners, chunks, order...]
where the time goes in v5:
time: 73.1 us; the launch traced here: 72.9 us
  Pallas kernels  72.3 us (99%)
    pallas_call x1, Pallas kernels, shards(): pl.pallas_call(functools.partial(kernel, dp, peers, owners, chunks, order...  69.1 us
    pallas_call x1, Pallas kernels, shards(): pl.pallas_call(widen, out_shape=(master,) * 3 + (jax.ShapeDtypeStruct((ne...  3.14 us

profile of v5, /device:TPU:0, one launch (start us, length us, event | category | flops | bytes accessed | tf_op | source)
XLA Modules:
  0.0 72.9 jit_solution(10901069959097892926)
XLA Ops:
  0.6 69.1 %shard_map.93 = (bf16[2,6,128,512]{3,2,1,0:T(8,128)(2,1)S(1)}, bf16[6,128,2048]{2,1,0:T(8,128)(2,1)S(1)}) custom-call(s32[28]{0:T(128)} %old_ref.1, s32[28]{0:T(128)} %new_ref.1, bf16[1,4,128,2048]{3,2,1,0:T(8,128)(2,1)} %g_hbm.1, f32[4,128,512]{2,1,0:T(8,128)} %m_hbm.1, f32[4,128,512]{2,1,0:T(8,128)} %v_hbm.1, f32[4,128,512]{2,1,0:T(8,128)} %w_hbm.1), custom_call_target="tpu_custom_call" | custom-call | tf_op jit(solution)/shard_map/pallas_call | solution.py:458
  69.8 3.1 %shard_map.94 = (f32[6,128,512]{2,1,0:T(8,128)}, f32[6,128,512]{2,1,0:T(8,128)}, f32[6,128,512]{2,1,0:T(8,128)}, bf16[6,128,2048]{2,1,0:T(8,128)(2,1)}) custom-call(bf16[2,6,128,512]{3,2,1,0:T(8,128)(2,1)S(1)} %get-tuple-element.6.moments, bf16[6,128,2048]{2,1,0:T(8,128)(2,1)S(1)} %get-tuple-element.7.params), custom_call_target="tpu_custom_call" | custom-call | tf_op jit(solution)/shard_map/pallas_call | solution.py:471

commit v6 on v5

--- a/solution.py
+++ b/solution.py
@@ -11,24 +11,27 @@
 MESH = pl.DeviceIdType.MESH
 ROWS = 16
 KINDS = 'UDXMWFVZA'
-PARTS = (2, 2, 2, 1, 1, 1, 1, 1)
-EARLY = (0, 0, 1, 0, 1, 1, 1, 1, 0, 1, 0)
-SPLIT = (0, 0, 0, 0, 0, 0, 0, 0, 0, 0, 0)
-AHEAD = (0, 1, 0, 0, 0, 0, 0, 0, 1, 0, 1)
+PARTS = (2, 2, 2, 1, 1, 1, 1, 2)
+EARLY = (1, 1, 0, 0, 1, 0, 1, 1, 1, 0, 1, 0)
+SPLIT = (0, 0, 0, 0, 0, 0, 0, 0, 0, 1, 0, 0)
+AHEAD = (1, 1, 0, 1, 1, 1, 1, 1, 1, 0, 1, 1)
 ORDERS = (
     (
-        12, 23, 8080, 43, 22, 8010, 3, 11, 8100, 33, 13, 2, 21, 42, 53, 63, 1, 41, 2020, 2040, 3020, 3040, 32,
-        2000, 62, 2030, 73, 3030, 31, 3000, 61, 2050, 52, 3050, 83, 82, 2010, 51, 3010, 2060, 81, 103, 3060, 93,
-        4020, 4040, 72, 92, 2070, 3070, 71, 91, 6030, 6020, 6000, 2080, 102, 3080, 4050, 6010, 2100, 3100, 2090,
-        4060, 101, 6040, 6050, 3090, 6080, 6100, 4070, 4090, 7000, 6070, 7010, 7030, 6060, 6090, 7080, 7100,
+        33, 8080, 3, 8050, 13, 22, 43, 23, 2, 8030, 12, 8070, 8100, 63, 8010, 21, 1, 52, 8000, 11, 53, 8040,
+        2000, 2010, 3000, 42, 2030, 51, 83, 3010, 41, 113, 62, 2040, 2020, 112, 32, 61, 103, 8060, 3040, 31,
+        3020, 2060, 3030, 93, 4000, 3060, 8110, 73, 2050, 111, 2110, 4010, 2080, 72, 3050, 3110, 82, 102, 4040,
+        92, 71, 81, 3080, 6040, 91, 101, 4060, 6010, 6000, 6030, 2090, 2070, 4090, 6020, 3070, 6050, 2100, 6090,
+        3090, 6110, 3100, 4080, 6060, 4070, 4100, 6070, 7050, 6080, 7090, 7020, 7030, 6100, 7110,
     ),
     (
-        12, 8010, 23, 43, 3, 22, 8100, 2010, 3010, 33, 1020, 1040, 13, 1000, 2, 2020, 42, 1030, 53, 3020, 1010,
-        6010, 5022, 63, 8080, 2000, 3000, 2040, 5040, 1050, 5012, 3040, 32, 5020, 1060, 62, 5042, 5043, 4040,
-        6000, 73, 2030, 3030, 5023, 2060, 52, 5050, 5002, 3060, 83, 1070, 4020, 82, 6030, 2050, 3050, 5053,
-        5060, 1080, 5062, 2080, 103, 3080, 5032, 93, 6020, 5052, 5063, 4060, 72, 1100, 4050, 92, 1090, 5070,
-        6080, 2090, 6040, 3090, 5073, 2070, 6060, 102, 3070, 5030, 5082, 5090, 5072, 2100, 5092, 3100, 5000,
-        5033, 5010, 4070, 5080, 5093, 5003, 4090, 5013, 5100, 6100, 5083, 6050, 5103, 5102, 6070, 6090,
+        8000, 8030, 8060, 8100, 33, 8110, 3, 8050, 13, 8080, 22, 43, 1030, 23, 1000, 2, 1010, 12, 1040, 8010,
+        63, 2020, 3020, 1020, 2000, 52, 3000, 8040, 8070, 2010, 53, 1060, 5000, 5010, 5002, 42, 6020, 3010,
+        1050, 2050, 5003, 83, 3050, 4000, 5013, 5012, 113, 2040, 5022, 62, 3040, 4010, 1080, 5040, 32, 1110,
+        6050, 2060, 103, 5043, 5042, 112, 2030, 3030, 3060, 4040, 5060, 5052, 5062, 93, 73, 1100, 6030, 2110,
+        5063, 3110, 1090, 5080, 4060, 72, 1070, 6040, 5032, 82, 92, 5083, 6000, 102, 2070, 3070, 2080, 6010,
+        6110, 2090, 4090, 2100, 3090, 5072, 5082, 5070, 5112, 3080, 6090, 4080, 5100, 5050, 5020, 7090, 5073,
+        5090, 6060, 3100, 5110, 4070, 5092, 5103, 5102, 4100, 5030, 5053, 5023, 6080, 5093, 5033, 5113, 6070,
+        6100,
     ),
 )
 

time: 73.1 us -> 72.1 us (0.986)
  Pallas kernels: 72.3 us -> 71.3 us
    pallas_call x1, Pallas kernels: 69.1 us -> 68.2 us  [shards(): pl.pallas_call(functools.partial(kernel, dp, peers, owners, chunks, order...]
where the time goes in v6:
time: 72.1 us; the launch traced here: 72 us
  Pallas kernels  71.3 us (99%)
    pallas_call x1, Pallas kernels, shards(): pl.pallas_call(functools.partial(kernel, dp, peers, owners, chunks, order...  68.2 us
    pallas_call x1, Pallas kernels, shards(): pl.pallas_call(widen, out_shape=(master,) * 3 + (jax.ShapeDtypeStruct((ne...  3.14 us

profile of v6, /device:TPU:0, one launch (start us, length us, event | category | flops | bytes accessed | tf_op | source)
XLA Modules:
  0.0 72.0 jit_solution(10488842235947805865)
XLA Ops:
  0.6 68.2 %shard_map.93 = (bf16[2,6,128,512]{3,2,1,0:T(8,128)(2,1)S(1)}, bf16[6,128,2048]{2,1,0:T(8,128)(2,1)S(1)}) custom-call(s32[28]{0:T(128)} %old_ref.1, s32[28]{0:T(128)} %new_ref.1, bf16[1,4,128,2048]{3,2,1,0:T(8,128)(2,1)} %g_hbm.1, f32[4,128,512]{2,1,0:T(8,128)} %m_hbm.1, f32[4,128,512]{2,1,0:T(8,128)} %v_hbm.1, f32[4,128,512]{2,1,0:T(8,128)} %w_hbm.1), custom_call_target="tpu_custom_call" | custom-call | tf_op jit(solution)/shard_map/pallas_call | solution.py:461
  68.8 3.1 %shard_map.94 = (f32[6,128,512]{2,1,0:T(8,128)}, f32[6,128,512]{2,1,0:T(8,128)}, f32[6,128,512]{2,1,0:T(8,128)}, bf16[6,128,2048]{2,1,0:T(8,128)(2,1)}) custom-call(bf16[2,6,128,512]{3,2,1,0:T(8,128)(2,1)S(1)} %get-tuple-element.6.moments, bf16[6,128,2048]{2,1,0:T(8,128)(2,1)S(1)} %get-tuple-element.7.params), custom_call_target="tpu_custom_call" | custom-call | tf_op jit(solution)/shard_map/pallas_call | solution.py:474

commit v7 on v6

--- a/solution.py
+++ b/solution.py
@@ -13,25 +13,25 @@
 KINDS = 'UDXMWFVZA'
 PARTS = (2, 2, 2, 1, 1, 1, 1, 2)
 EARLY = (1, 1, 0, 0, 1, 0, 1, 1, 1, 0, 1, 0)
-SPLIT = (0, 0, 0, 0, 0, 0, 0, 0, 0, 1, 0, 0)
-AHEAD = (1, 1, 0, 1, 1, 1, 1, 1, 1, 0, 1, 1)
+SPLIT = (0, 0, 0, 1, 0, 0, 0, 0, 0, 1, 0, 0)
+AHEAD = (1, 1, 0, 0, 1, 1, 1, 1, 1, 0, 1, 1)
 ORDERS = (
     (
-        33, 8080, 3, 8050, 13, 22, 43, 23, 2, 8030, 12, 8070, 8100, 63, 8010, 21, 1, 52, 8000, 11, 53, 8040,
-        2000, 2010, 3000, 42, 2030, 51, 83, 3010, 41, 113, 62, 2040, 2020, 112, 32, 61, 103, 8060, 3040, 31,
-        3020, 2060, 3030, 93, 4000, 3060, 8110, 73, 2050, 111, 2110, 4010, 2080, 72, 3050, 3110, 82, 102, 4040,
-        92, 71, 81, 3080, 6040, 91, 101, 4060, 6010, 6000, 6030, 2090, 2070, 4090, 6020, 3070, 6050, 2100, 6090,
-        3090, 6110, 3100, 4080, 6060, 4070, 4100, 6070, 7050, 6080, 7090, 7020, 7030, 6100, 7110,
+        33, 13, 3, 53, 22, 8070, 23, 8080, 8100, 2, 63, 12, 8060, 21, 43, 1, 52, 8110, 8010, 8000, 2030, 8040,
+        2010, 11, 2000, 3010, 51, 42, 32, 83, 62, 8050, 41, 103, 113, 61, 2050, 2020, 3020, 3050, 31, 3030,
+        3000, 2040, 2060, 3040, 4000, 4010, 73, 93, 4030, 72, 112, 3060, 71, 82, 2080, 111, 81, 3080, 102, 6000,
+        2110, 4040, 92, 6030, 4060, 2100, 101, 3110, 2090, 6040, 2070, 91, 4090, 3070, 6020, 6050, 6110, 3100,
+        4080, 6090, 6060, 4100, 4070, 7020, 6080, 3090, 6100, 6010, 7110, 6070, 7050, 7030, 7090,
     ),
     (
-        8000, 8030, 8060, 8100, 33, 8110, 3, 8050, 13, 8080, 22, 43, 1030, 23, 1000, 2, 1010, 12, 1040, 8010,
-        63, 2020, 3020, 1020, 2000, 52, 3000, 8040, 8070, 2010, 53, 1060, 5000, 5010, 5002, 42, 6020, 3010,
-        1050, 2050, 5003, 83, 3050, 4000, 5013, 5012, 113, 2040, 5022, 62, 3040, 4010, 1080, 5040, 32, 1110,
-        6050, 2060, 103, 5043, 5042, 112, 2030, 3030, 3060, 4040, 5060, 5052, 5062, 93, 73, 1100, 6030, 2110,
-        5063, 3110, 1090, 5080, 4060, 72, 1070, 6040, 5032, 82, 92, 5083, 6000, 102, 2070, 3070, 2080, 6010,
-        6110, 2090, 4090, 2100, 3090, 5072, 5082, 5070, 5112, 3080, 6090, 4080, 5100, 5050, 5020, 7090, 5073,
-        5090, 6060, 3100, 5110, 4070, 5092, 5103, 5102, 4100, 5030, 5053, 5023, 6080, 5093, 5033, 5113, 6070,
-        6100,
+        8080, 8110, 8000, 8060, 8050, 8070, 33, 13, 8010, 3, 53, 8040, 22, 1030, 23, 1010, 2, 1000, 63, 12,
+        1050, 2020, 3020, 1020, 43, 2000, 52, 1060, 5010, 3000, 2010, 5000, 1040, 6020, 2050, 3050, 5002, 8100,
+        42, 5012, 5013, 4010, 32, 5003, 83, 3010, 5022, 4000, 62, 6050, 2040, 113, 3040, 1080, 103, 2060, 2030,
+        4030, 5052, 3030, 5040, 5042, 3060, 5060, 1110, 73, 1100, 5062, 5043, 4040, 93, 5063, 72, 1070, 6030,
+        112, 4060, 82, 1090, 2070, 2110, 7030, 3110, 5032, 5080, 3070, 2080, 102, 3080, 6000, 92, 5072, 5030,
+        6040, 5083, 5100, 5082, 2100, 5070, 3100, 6110, 2090, 4090, 6010, 5033, 5103, 5020, 6060, 5102, 4100,
+        5073, 5110, 4080, 4070, 6090, 5113, 6100, 5050, 5090, 3090, 5023, 5092, 5112, 5053, 6080, 5093, 6070,
+        7090,
     ),
 )
 
@@ -84,18 +84,20 @@
         orders = [
             [(KINDS[code // 1000], code // 10 % 100, code % 10) for code in coded] for coded in ORDERS
         ]
+    start = [job[0] == "X" for job in orders[0]].index(True)
+    orders[0][:start] = sorted(orders[0][:start], key=lambda job: job[0] != "U")
     return chunks, orders
 
 
 def kernel(dp, peers, owners, chunks, orders, old_ref, new_ref, g_hbm, m_hbm, v_hbm, w_hbm, *rest):
     moments, params, rest = rest[0], rest[1], rest[2:]
-    g, state, part, line = rest[:4]
-    rest = rest[4:]
+    g, state, weights, part, line = rest[:5]
+    rest = rest[5:]
     count = len(chunks)
     fresh, mail, inbox, wide, wide_mail, wide_inbox, old_mail, old_inbox = (
         rest[i * count : (i + 1) * count] for i in range(8)
     )
-    g_sem, in_sem, sent, z_recv, x_recv, w_recv, o_recv = rest[8 * count :]
+    g_sem, old_sem, in_sem, sent, z_recv, x_recv, w_recv, o_recv = rest[8 * count :]
     z = lax.axis_index("dp")
     e = lax.axis_index("expert")
     old_slots, cols = state.shape[1], state.shape[-1]
@@ -140,7 +142,8 @@
         pltpu.make_async_copy(g_hbm.at[0, :, pl.ds(row, ROWS)], g.at[:, pl.ds(row, ROWS)], g_sem.at[row // ROWS])
         for row in range(0, g.shape[1], ROWS)
     ]
-    loads = [pltpu.make_async_copy(ref, state.at[i], in_sem) for i, ref in enumerate((m_hbm, v_hbm, w_hbm))]
+    loads = [pltpu.make_async_copy(w_hbm, weights, old_sem)]
+    loads += [pltpu.make_async_copy(ref, state.at[i], in_sem) for i, ref in enumerate((m_hbm, v_hbm))]
 
     @pl.when(owns)
     def _():
@@ -156,7 +159,7 @@
 
     @pl.when(owns)
     def _():
-        for load in loads + g_loads[1:]:
+        for load in g_loads[1:3] + loads[:1] + g_loads[3:] + loads[1:]:
             load.start()
 
     inner = (z > 0).astype(jnp.int32) + (z < dp - 1).astype(jnp.int32)
@@ -247,7 +250,7 @@
                 gradient += line[way(right), z, slot, rows(c), span(c)].astype(jnp.float32)
             values = list(moment_step(gradient, *(state[i, slot, rows(c), span(c)] for i in range(2))))
             if chunks[c].early or not chunks[c].ahead:
-                values.insert(0, weight_step(*values, state[2, slot, rows(c), span(c)]))
+                values.insert(0, weight_step(*values, weights[slot, rows(c), span(c)]))
             values = [value.astype(jnp.bfloat16) for value in values]
             if chunks[c].early:
                 wide[c][slot, :, pl.ds(0, chunks[c].width)] = values.pop(0)
@@ -270,9 +273,9 @@
 
     def post_old_weights(c, slots):
         for to, slot in zip(targets[1:], slots[1:]):
-            old_mail[c][to] = state[2, slot, rows(c), span(c)].astype(jnp.bfloat16)
+            old_mail[c][to] = weights[slot, rows(c), span(c)].astype(jnp.bfloat16)
             old_copy(c, to).start()
-        old_inbox[c][e] = state[2, slots[0], rows(c), span(c)].astype(jnp.bfloat16)
+        old_inbox[c][e] = weights[slots[0], rows(c), span(c)].astype(jnp.bfloat16)
 
     def post_weights(c, role, slots):
         if chunks[c].early:
@@ -342,6 +345,9 @@
                     g_loads[chunks[c].row // ROWS].wait()
                 if kind in "XA" and -1 not in loaded:
                     loaded.append(-1)
+                    loads[0].wait()
+                if kind == "X" and -2 not in loaded:
+                    loaded.append(-2)
                     taken_by(in_sem, state)
                 if kind == "U" and role == 0:
                     sum_copy(c, k, True, True).start()
@@ -369,7 +375,7 @@
                 job()
 
     lead = 0
-    while orders[0][lead][:2] == ("U", 0):
+    while orders[0][lead][0] == "U":
         lead += 1
     loaded = [[] for _ in orders]
 
@@ -443,7 +449,8 @@
     master = jax.ShapeDtypeStruct((new_slots, tile_rows, cols), f32)
     scratch = [
         pltpu.VMEM((old_slots, tile_rows, dp * cols), bf16),
-        pltpu.VMEM((3, old_slots, tile_rows, cols), f32),
+        pltpu.VMEM((2, old_slots, tile_rows, cols), f32),
+        pltpu.VMEM((old_slots, tile_rows, cols), f32),
         pltpu.VMEM((dp, old_slots, tile_rows, cols), bf16),
         pltpu.VMEM((2, dp, old_slots, tile_rows, cols), bf16),
     ]
@@ -455,7 +462,7 @@
         scratch += [pltpu.VMEM((boxes, n, ROWS, chunk.width), bf16) for n, chunk in zip(kept, chunks)]
     for boxes, sizes in ((old_slots, wide), (peers, sent), (owners, sent), (peers, old), (owners, old)):
         scratch += [pltpu.VMEM((boxes, ROWS, n), bf16) for n in sizes]
-    scratch += [dma((tile_rows // ROWS,)), dma, dma, dma((count, dp))]
+    scratch += [dma((tile_rows // ROWS,)), dma, dma, dma, dma((count, dp))]
     scratch += [dma((count,))] * 3
     results = new_slots * tile_rows * cols * (4 + 2 * dp)
     moments, params = pl.pallas_call(

time: 72.1 us -> 71.9 us (level)
  no operation moved by 1% of the time
where the time goes in v7:
time: 71.9 us; the launch traced here: 71.8 us
  Pallas kernels  71.1 us (99%)
    pallas_call x1, Pallas kernels, shards(): pl.pallas_call(functools.partial(kernel, dp, peers, owners, chunks, order...  68 us
    pallas_call x1, Pallas kernels, shards(): pl.pallas_call(widen, out_shape=(master,) * 3 + (jax.ShapeDtypeStruct((ne...  3.14 us

profile of v7, /device:TPU:0, one launch (start us, length us, event | category | flops | bytes accessed | tf_op | source)
XLA Modules:
  0.0 71.8 jit_solution(10659333827233281363)
XLA Ops:
  0.6 68.0 %shard_map.93 = (bf16[2,6,128,512]{3,2,1,0:T(8,128)(2,1)S(1)}, bf16[6,128,2048]{2,1,0:T(8,128)(2,1)S(1)}) custom-call(s32[28]{0:T(128)} %old_ref.1, s32[28]{0:T(128)} %new_ref.1, bf16[1,4,128,2048]{3,2,1,0:T(8,128)(2,1)} %g_hbm.1, f32[4,128,512]{2,1,0:T(8,128)} %m_hbm.1, f32[4,128,512]{2,1,0:T(8,128)} %v_hbm.1, f32[4,128,512]{2,1,0:T(8,128)} %w_hbm.1), custom_call_target="tpu_custom_call" | custom-call | tf_op jit(solution)/shard_map/pallas_call | solution.py:468
  68.6 3.1 %shard_map.94 = (f32[6,128,512]{2,1,0:T(8,128)}, f32[6,128,512]{2,1,0:T(8,128)}, f32[6,128,512]{2,1,0:T(8,128)}, bf16[6,128,2048]{2,1,0:T(8,128)(2,1)}) custom-call(bf16[2,6,128,512]{3,2,1,0:T(8,128)(2,1)S(1)} %get-tuple-element.6.moments, bf16[6,128,2048]{2,1,0:T(8,128)(2,1)S(1)} %get-tuple-element.7.params), custom_call_target="tpu_custom_call" | custom-call | tf_op jit(solution)/shard_map/pallas_call | solution.py:481

commit v8 on v7

--- a/solution.py
+++ b/solution.py
@@ -13,25 +13,24 @@
 KINDS = 'UDXMWFVZA'
 PARTS = (2, 2, 2, 1, 1, 1, 1, 2)
 EARLY = (1, 1, 0, 0, 1, 0, 1, 1, 1, 0, 1, 0)
-SPLIT = (0, 0, 0, 1, 0, 0, 0, 0, 0, 1, 0, 0)
+SPLIT = (0, 0, 1, 0, 0, 0, 0, 0, 0, 1, 0, 0)
 AHEAD = (1, 1, 0, 0, 1, 1, 1, 1, 1, 0, 1, 1)
 ORDERS = (
     (
-        33, 13, 3, 53, 22, 8070, 23, 8080, 8100, 2, 63, 12, 8060, 21, 43, 1, 52, 8110, 8010, 8000, 2030, 8040,
-        2010, 11, 2000, 3010, 51, 42, 32, 83, 62, 8050, 41, 103, 113, 61, 2050, 2020, 3020, 3050, 31, 3030,
-        3000, 2040, 2060, 3040, 4000, 4010, 73, 93, 4030, 72, 112, 3060, 71, 82, 2080, 111, 81, 3080, 102, 6000,
-        2110, 4040, 92, 6030, 4060, 2100, 101, 3110, 2090, 6040, 2070, 91, 4090, 3070, 6020, 6050, 6110, 3100,
-        4080, 6090, 6060, 4100, 4070, 7020, 6080, 3090, 6100, 6010, 7110, 6070, 7050, 7030, 7090,
+        3, 8080, 8060, 43, 13, 23, 8110, 22, 63, 33, 8000, 42, 8070, 2, 53, 12, 8040, 8050, 21, 41, 8100, 52, 1,
+        11, 2040, 8010, 2010, 3010, 51, 83, 2000, 103, 2020, 3020, 62, 113, 2060, 32, 61, 31, 3000, 3060, 2030,
+        93, 72, 112, 3030, 73, 4040, 2050, 82, 71, 3050, 4010, 111, 2080, 4000, 81, 3080, 4020, 102, 2100, 2110,
+        3110, 92, 4060, 6020, 3040, 6050, 2090, 101, 6010, 6000, 4090, 3090, 2070, 91, 3070, 3100, 6060, 6110,
+        6030, 6090, 6040, 4080, 4100, 4070, 7030, 7110, 7050, 6080, 6100, 7020, 6070, 7090,
     ),
     (
-        8080, 8110, 8000, 8060, 8050, 8070, 33, 13, 8010, 3, 53, 8040, 22, 1030, 23, 1010, 2, 1000, 63, 12,
-        1050, 2020, 3020, 1020, 43, 2000, 52, 1060, 5010, 3000, 2010, 5000, 1040, 6020, 2050, 3050, 5002, 8100,
-        42, 5012, 5013, 4010, 32, 5003, 83, 3010, 5022, 4000, 62, 6050, 2040, 113, 3040, 1080, 103, 2060, 2030,
-        4030, 5052, 3030, 5040, 5042, 3060, 5060, 1110, 73, 1100, 5062, 5043, 4040, 93, 5063, 72, 1070, 6030,
-        112, 4060, 82, 1090, 2070, 2110, 7030, 3110, 5032, 5080, 3070, 2080, 102, 3080, 6000, 92, 5072, 5030,
-        6040, 5083, 5100, 5082, 2100, 5070, 3100, 6110, 2090, 4090, 6010, 5033, 5103, 5020, 6060, 5102, 4100,
-        5073, 5110, 4080, 4070, 6090, 5113, 6100, 5050, 5090, 3090, 5023, 5092, 5112, 5053, 6080, 5093, 6070,
-        7090,
+        3, 8110, 43, 8070, 13, 22, 1000, 8050, 8060, 23, 8100, 1040, 8000, 8010, 63, 1010, 8080, 33, 42, 1020,
+        53, 2, 1060, 12, 2020, 4020, 1030, 2040, 52, 3020, 8040, 1050, 2000, 2010, 5040, 3000, 5010, 6020, 2050,
+        3050, 5042, 3040, 5002, 83, 5043, 5012, 4040, 5000, 3010, 5013, 103, 5022, 62, 6050, 5003, 1080, 4010,
+        32, 1100, 5060, 113, 2060, 3060, 2030, 5052, 3030, 93, 5063, 1110, 72, 5062, 4000, 4060, 112, 73, 1090,
+        6030, 82, 2070, 2110, 3110, 1070, 5080, 3070, 5032, 2080, 102, 5072, 3080, 6000, 5100, 92, 6110, 5082,
+        6040, 2100, 5083, 4080, 5070, 5103, 5020, 2090, 4090, 5112, 6060, 5102, 5110, 4100, 5073, 5030, 5023,
+        5050, 5090, 4070, 5113, 6080, 5033, 3100, 6010, 6090, 5053, 5093, 3090, 5092, 7020, 6100, 6070, 7090,
     ),
 )
 

time: 71.9 us -> 72 us (level)
  no operation moved by 1% of the time
where the time goes in v8:
time: 72 us; the launch traced here: 71.8 us
  Pallas kernels  71.2 us (99%)
    pallas_call x1, Pallas kernels, shards(): pl.pallas_call(functools.partial(kernel, dp, peers, owners, chunks, order...  68 us
    pallas_call x1, Pallas kernels, shards(): pl.pallas_call(widen, out_shape=(master,) * 3 + (jax.ShapeDtypeStruct((ne...  3.14 us

profile of v8, /device:TPU:0, one launch (start us, length us, event | category | flops | bytes accessed | tf_op | source)
XLA Modules:
  0.0 71.8 jit_solution(2144201294096742342)
XLA Ops:
  0.6 68.0 %shard_map.93 = (bf16[2,6,128,512]{3,2,1,0:T(8,128)(2,1)S(1)}, bf16[6,128,2048]{2,1,0:T(8,128)(2,1)S(1)}) custom-call(s32[28]{0:T(128)} %old_ref.1, s32[28]{0:T(128)} %new_ref.1, bf16[1,4,128,2048]{3,2,1,0:T(8,128)(2,1)} %g_hbm.1, f32[4,128,512]{2,1,0:T(8,128)} %m_hbm.1, f32[4,128,512]{2,1,0:T(8,128)} %v_hbm.1, f32[4,128,512]{2,1,0:T(8,128)} %w_hbm.1), custom_call_target="tpu_custom_call" | custom-call | tf_op jit(solution)/shard_map/pallas_call | solution.py:467
  68.7 3.1 %shard_map.94 = (f32[6,128,512]{2,1,0:T(8,128)}, f32[6,128,512]{2,1,0:T(8,128)}, f32[6,128,512]{2,1,0:T(8,128)}, bf16[6,128,2048]{2,1,0:T(8,128)(2,1)}) custom-call(bf16[2,6,128,512]{3,2,1,0:T(8,128)(2,1)S(1)} %get-tuple-element.6.moments, bf16[6,128,2048]{2,1,0:T(8,128)(2,1)S(1)} %get-tuple-element.7.params), custom_call_target="tpu_custom_call" | custom-call | tf_op jit(solution)/shard_map/pallas_call | solution.py:480
